TPU v7x, 512 devices: a whole 4x8x8 slice. The times are simulated.
512 devices in a mesh: gx: 32 (over y_hi, z, core), yz: 16 (over x, y_lo).
Axes of the slice: x: 4, y: 8 (y_hi: 2, y_lo: 4; y = y_hi * 4 + y_lo), z: 8, core: 2. Of those that a mesh axis runs over, the one named last changes fastest.
Arguments:
- gauge_links: float32 [64, 2, 3, 3, 2048], P('gx', None, None, None, 'yz'), may hold values from -1 to 1, as said below
- in_field: float32 [8, 64, 2, 3, 3, 2048], P(None, 'gx', None, None, None, 'yz'), may hold values from -6 to 6
- cotangent: float32 [8, 64, 2, 3, 3, 2048], P(None, 'gx', None, None, None, 'yz'), may hold values from -6 to 6
- bilinear_weights: float32 [8, 8, 24, 8], replicated, may hold values from -0.15625 to 0.15625
Outputs:
- grad_field: float32 [8, 64, 2, 3, 3, 2048], P(None, 'gx', None, None, None, 'yz')
- grad_weights: float32 [8, 8, 24, 8], replicated
Inputs may be any that keep to these rules, and one draw needn't show every extreme that they name: `gauge_links`: every site's link is a special unitary 3 x 3 matrix (unitary with determinant 1), stored as real and imaginary parts.
All inputs are finite; a program needn't handle non-finite values.
Results may differ from a plain program's by a relative error of at most 0.0003.
Values sent between devices are 32-bit elements; how exact they have to be, the bound alone decides.
No kernel may reach another device: no remote copies, remote signals or barrier semaphores. Data moves between devices by JAX's collectives and lax.ppermute only.
A program may use at most 64 MiB of HBM per device.

v0:
```python
import math

import jax
import jax.numpy as jnp
from jax import lax
from jax.sharding import PartitionSpec as P


def from_behind(block, axis, distance):
    devices = range(lax.axis_size(axis))
    route = [((i - distance) % len(devices), i) for i in devices]
    return lax.ppermute(block, axis, route)


def matmul_three(left, right):
    return jnp.sum(left[..., :, :, None, :] * right[..., None, :, :, :], axis=-3)


def complex_mul(left, right):
    left_re = left[..., 0, :, :, :]
    left_im = left[..., 1, :, :, :]
    right_re = right[..., 0, :, :, :]
    right_im = right[..., 1, :, :, :]
    real_part = matmul_three(left_re, right_re) - matmul_three(left_im, right_im)
    imag_part = matmul_three(left_re, right_im) + matmul_three(left_im, right_re)
    return jnp.stack([real_part, imag_part], axis=-4)


def dagger(matrix):
    swapped = jnp.swapaxes(matrix, -3, -2)
    return jnp.stack([swapped[..., 0, :, :, :], -swapped[..., 1, :, :, :]], axis=-4)


def per_device(gauge_links, in_field, cotangent, bilinear_weights):
    part_x = gauge_links.shape[0]
    channels = in_field.shape[0]
    line_count = bilinear_weights.shape[2]
    site_count = gauge_links.shape[-1]
    reach_devs = (part_x - 1 + line_count) // part_x
    highest = lax.Precision.HIGHEST
    weight_rows = bilinear_weights.reshape(channels * channels, line_count * channels)

    def advance(carry, unused):
        arrived = from_behind(carry, "gx", -1)
        return (arrived, arrived)

    unused_last, stacked = lax.scan(advance, (gauge_links, in_field), None, length=reach_devs)
    window_links = jnp.concatenate(
        [gauge_links, stacked[0].reshape((-1, 2, 3, 3, site_count))], axis=0
    )
    later_field = jnp.moveaxis(stacked[1], 0, 1).reshape((channels, -1, 2, 3, 3, site_count))
    window_field = jnp.concatenate([in_field, later_field], axis=1)
    pair_grad = complex_mul(dagger(in_field)[None], cotangent[:, None]).reshape(
        channels * channels, -1
    )

    def forward_step(line, offset):
        shifted = lax.dynamic_slice_in_dim(window_field, offset, part_x, axis=1)
        transported = complex_mul(complex_mul(line[None], shifted), dagger(line)[None])
        next_links = lax.dynamic_slice_in_dim(window_links, offset, part_x, axis=0)
        return (complex_mul(line, next_links), (transported, line))

    offsets = jnp.arange(1, line_count + 1, dtype=jnp.int32)
    unused_line, (all_transported, all_lines) = lax.scan(forward_step, gauge_links, offsets)
    transported_flat = all_transported.reshape(line_count * channels, -1)
    partial_grad = lax.dot_general(
        pair_grad, transported_flat, (((1,), (1,)), ((), ())), precision=highest
    )
    mixed = jnp.dot(weight_rows, transported_flat, precision=highest)
    mixed_matrix = mixed.reshape((channels, channels) + in_field.shape[1:])
    direct = jnp.sum(complex_mul(cotangent[:, None], dagger(mixed_matrix)), axis=0)
    line_grad = jnp.dot(weight_rows.T, pair_grad, precision=highest)
    line_grad = line_grad.reshape((line_count,) + in_field.shape)
    accumulator = jnp.zeros((channels, (reach_devs + 1) * part_x, 2, 3, 3, site_count), jnp.float32)

    def backward_step(carry, inputs):
        offset, grad_piece, line = inputs
        contribution = complex_mul(complex_mul(dagger(line)[None], grad_piece), line[None])
        current = lax.dynamic_slice_in_dim(carry, offset, part_x, axis=1)
        return (
            lax.dynamic_update_slice_in_dim(carry, current + contribution, offset, axis=1),
            None,
        )

    accumulator, unused_out = lax.scan(backward_step, accumulator, (offsets, line_grad, all_lines))
    blocks = jnp.moveaxis(
        accumulator.reshape((channels, reach_devs + 1, part_x, 2, 3, 3, site_count)), 1, 0
    )

    def return_step(carry, block):
        arrived = from_behind(carry, "gx", 1)
        return (arrived + block, None)

    far_terms, unused_tail = lax.scan(return_step, blocks[reach_devs], blocks[:reach_devs][::-1])
    grad_field = direct + far_terms
    total_x = part_x * lax.axis_size("gx")
    total_sites = site_count * lax.axis_size("yz")
    summed = lax.psum(partial_grad, ("gx", "yz"))
    grad_weights = summed.reshape(channels, channels, line_count, channels) / math.sqrt(
        100.0 * total_x * total_sites
    )
    return (grad_field, grad_weights)


def solution(mesh):
    placed = (
        P("gx", None, None, None, "yz"),
        P(None, "gx", None, None, None, "yz"),
        P(None, "gx", None, None, None, "yz"),
        P(),
    )
    return jax.shard_map(
        per_device,
        mesh=mesh,
        in_specs=placed,
        out_specs=(P(None, "gx", None, None, None, "yz"), P()),
        check_vma=False,
    )
```

profile of v0, /device:TPU:2, one launch (start us, length us, event | category | flops | bytes accessed | tf_op | source)
XLA Modules:
  0.0 771.0 jit_solution(7964423564091880756)
XLA Ops:
  2.4 183.7 %while.50 = (s32[]{:T(128)}, f32[2,2,3,3,128]{4,1,3,2,0:T(2,128)S(1)}, f32[8,2,2,3,3,128]{5,2,4,3,1,0:T(2,128)S(1)}, f32[12,2,2,3,3,128]{5,1,0,4,3,2:T(2,128)S(1...) while((s32[]{:T(128)}, f32[2,2,3,3,128]{4,1,3,2,0:T(2,128)S(1)}, ...), condition=%wide.region_1.2_spmd, body=%wide.region_0.1_spmd.sunk | while | flops 2 | bytes 1327269 | solution.py:47
  2.4 15.6 %collective-permute-start = (f32[2,2,3,3,128]{4,1,3,2,0:T(2,128)S(1)}, f32[2,2,3,3,128]{4,1,3,2,0:T(2,128)S(1)}, u32[]{:S(2)}, u32[]{:S(2)}) collective-permute-start(f32[2,2,3,3,128]{4,1,3,2,0:T(2,128)S(1)} %get-tuple-element.507), channel_id=1, source_target_pairs={{16,0},{32,16},{48,32},{64,48},{80,64},{96,80},{112,96},{128,112},... | collective-permute-start | bytes 55304 | tf_op jit(solution)/shard_map/while/body/eval_jaxpr/ppermute | solution.py:12
  18.0 2.6 collective-permute-start.1
  20.6 4.2 collective-permute-done.1
  24.9 9.8 %collective-permute-start = (f32[2,2,3,3,128]{4,1,3,2,0:T(2,128)S(1)}, f32[2,2,3,3,128]{4,1,3,2,0:T(2,128)S(1)}, u32[]{:S(2)}, u32[]{:S(2)}) collective-permute-start(f32[2,2,3,3,128]{4,1,3,2,0:T(2,128)S(1)} %get-tuple-element.507), channel_id=1, source_target_pairs={{16,0},{32,16},{48,32},{64,48},{80,64},{96,80},{112,96},{128,112},... | collective-permute-start | bytes 55304 | tf_op jit(solution)/shard_map/while/body/eval_jaxpr/ppermute | solution.py:12
  34.7 1.9 collective-permute-start.1
  36.7 3.9 collective-permute-done.1
  40.8 9.8 %collective-permute-start = (f32[2,2,3,3,128]{4,1,3,2,0:T(2,128)S(1)}, f32[2,2,3,3,128]{4,1,3,2,0:T(2,128)S(1)}, u32[]{:S(2)}, u32[]{:S(2)}) collective-permute-start(f32[2,2,3,3,128]{4,1,3,2,0:T(2,128)S(1)} %get-tuple-element.507), channel_id=1, source_target_pairs={{16,0},{32,16},{48,32},{64,48},{80,64},{96,80},{112,96},{128,112},... | collective-permute-start | bytes 55304 | tf_op jit(solution)/shard_map/while/body/eval_jaxpr/ppermute | solution.py:12
  50.6 1.9 collective-permute-start.1
  52.6 2.7 collective-permute-done.1
  55.4 9.8 %collective-permute-start = (f32[2,2,3,3,128]{4,1,3,2,0:T(2,128)S(1)}, f32[2,2,3,3,128]{4,1,3,2,0:T(2,128)S(1)}, u32[]{:S(2)}, u32[]{:S(2)}) collective-permute-start(f32[2,2,3,3,128]{4,1,3,2,0:T(2,128)S(1)} %get-tuple-element.507), channel_id=1, source_target_pairs={{16,0},{32,16},{48,32},{64,48},{80,64},{96,80},{112,96},{128,112},... | collective-permute-start | bytes 55304 | tf_op jit(solution)/shard_map/while/body/eval_jaxpr/ppermute | solution.py:12
  65.2 1.9 collective-permute-start.1
  67.2 2.6 collective-permute-done.1
  69.9 9.8 %collective-permute-start = (f32[2,2,3,3,128]{4,1,3,2,0:T(2,128)S(1)}, f32[2,2,3,3,128]{4,1,3,2,0:T(2,128)S(1)}, u32[]{:S(2)}, u32[]{:S(2)}) collective-permute-start(f32[2,2,3,3,128]{4,1,3,2,0:T(2,128)S(1)} %get-tuple-element.507), channel_id=1, source_target_pairs={{16,0},{32,16},{48,32},{64,48},{80,64},{96,80},{112,96},{128,112},... | collective-permute-start | bytes 55304 | tf_op jit(solution)/shard_map/while/body/eval_jaxpr/ppermute | solution.py:12
  79.8 1.9 collective-permute-start.1
  81.7 2.6 collective-permute-done.1
  84.4 9.8 %collective-permute-start = (f32[2,2,3,3,128]{4,1,3,2,0:T(2,128)S(1)}, f32[2,2,3,3,128]{4,1,3,2,0:T(2,128)S(1)}, u32[]{:S(2)}, u32[]{:S(2)}) collective-permute-start(f32[2,2,3,3,128]{4,1,3,2,0:T(2,128)S(1)} %get-tuple-element.507), channel_id=1, source_target_pairs={{16,0},{32,16},{48,32},{64,48},{80,64},{96,80},{112,96},{128,112},... | collective-permute-start | bytes 55304 | tf_op jit(solution)/shard_map/while/body/eval_jaxpr/ppermute | solution.py:12
  94.3 1.9 collective-permute-start.1
  96.3 2.6 collective-permute-done.1
  99.0 9.8 %collective-permute-start = (f32[2,2,3,3,128]{4,1,3,2,0:T(2,128)S(1)}, f32[2,2,3,3,128]{4,1,3,2,0:T(2,128)S(1)}, u32[]{:S(2)}, u32[]{:S(2)}) collective-permute-start(f32[2,2,3,3,128]{4,1,3,2,0:T(2,128)S(1)} %get-tuple-element.507), channel_id=1, source_target_pairs={{16,0},{32,16},{48,32},{64,48},{80,64},{96,80},{112,96},{128,112},... | collective-permute-start | bytes 55304 | tf_op jit(solution)/shard_map/while/body/eval_jaxpr/ppermute | solution.py:12
  108.8 1.9 collective-permute-start.1
  110.8 2.6 collective-permute-done.1
  113.5 9.8 %collective-permute-start = (f32[2,2,3,3,128]{4,1,3,2,0:T(2,128)S(1)}, f32[2,2,3,3,128]{4,1,3,2,0:T(2,128)S(1)}, u32[]{:S(2)}, u32[]{:S(2)}) collective-permute-start(f32[2,2,3,3,128]{4,1,3,2,0:T(2,128)S(1)} %get-tuple-element.507), channel_id=1, source_target_pairs={{16,0},{32,16},{48,32},{64,48},{80,64},{96,80},{112,96},{128,112},... | collective-permute-start | bytes 55304 | tf_op jit(solution)/shard_map/while/body/eval_jaxpr/ppermute | solution.py:12
  123.3 1.9 collective-permute-start.1
  125.3 2.6 collective-permute-done.1
  128.0 9.8 %collective-permute-start = (f32[2,2,3,3,128]{4,1,3,2,0:T(2,128)S(1)}, f32[2,2,3,3,128]{4,1,3,2,0:T(2,128)S(1)}, u32[]{:S(2)}, u32[]{:S(2)}) collective-permute-start(f32[2,2,3,3,128]{4,1,3,2,0:T(2,128)S(1)} %get-tuple-element.507), channel_id=1, source_target_pairs={{16,0},{32,16},{48,32},{64,48},{80,64},{96,80},{112,96},{128,112},... | collective-permute-start | bytes 55304 | tf_op jit(solution)/shard_map/while/body/eval_jaxpr/ppermute | solution.py:12
  137.8 1.9 collective-permute-start.1
  139.8 2.6 collective-permute-done.1
  142.5 9.8 %collective-permute-start = (f32[2,2,3,3,128]{4,1,3,2,0:T(2,128)S(1)}, f32[2,2,3,3,128]{4,1,3,2,0:T(2,128)S(1)}, u32[]{:S(2)}, u32[]{:S(2)}) collective-permute-start(f32[2,2,3,3,128]{4,1,3,2,0:T(2,128)S(1)} %get-tuple-element.507), channel_id=1, source_target_pairs={{16,0},{32,16},{48,32},{64,48},{80,64},{96,80},{112,96},{128,112},... | collective-permute-start | bytes 55304 | tf_op jit(solution)/shard_map/while/body/eval_jaxpr/ppermute | solution.py:12
  152.3 1.9 collective-permute-start.1
  154.3 2.6 collective-permute-done.1
  157.0 9.8 %collective-permute-start = (f32[2,2,3,3,128]{4,1,3,2,0:T(2,128)S(1)}, f32[2,2,3,3,128]{4,1,3,2,0:T(2,128)S(1)}, u32[]{:S(2)}, u32[]{:S(2)}) collective-permute-start(f32[2,2,3,3,128]{4,1,3,2,0:T(2,128)S(1)} %get-tuple-element.507), channel_id=1, source_target_pairs={{16,0},{32,16},{48,32},{64,48},{80,64},{96,80},{112,96},{128,112},... | collective-permute-start | bytes 55304 | tf_op jit(solution)/shard_map/while/body/eval_jaxpr/ppermute | solution.py:12
  166.9 1.9 collective-permute-start.1
  168.9 2.6 collective-permute-done.1
  171.6 9.8 %collective-permute-start = (f32[2,2,3,3,128]{4,1,3,2,0:T(2,128)S(1)}, f32[2,2,3,3,128]{4,1,3,2,0:T(2,128)S(1)}, u32[]{:S(2)}, u32[]{:S(2)}) collective-permute-start(f32[2,2,3,3,128]{4,1,3,2,0:T(2,128)S(1)} %get-tuple-element.507), channel_id=1, source_target_pairs={{16,0},{32,16},{48,32},{64,48},{80,64},{96,80},{112,96},{128,112},... | collective-permute-start | bytes 55304 | tf_op jit(solution)/shard_map/while/body/eval_jaxpr/ppermute | solution.py:12
  181.4 1.9 collective-permute-start.1
  183.4 2.6 collective-permute-done.1
  189.8 184.4 %while.51 = (s32[]{:T(128)}, f32[2,2,3,3,128]{4,0,3,2,1:T(2,128)}, f32[24,8,2,2,3,3,128]{6,1,5,4,3,2,0:T(8,128)S(1)}, f32[24,2,2,3,3,128]{5,1,4,3,2,0:T(2,128)},...) while((s32[]{:T(128)}, f32[2,2,3,3,128]{4,0,3,2,1:T(2,128)}, ...), condition=%wide.region_15.16_spmd, body=%wide.region_2.15_spmd.sunk | while | flops 910086 | bytes 2968279 | solution.py:64
  374.2 2.1 copy.70
  376.3 2.0 reshape.184
  378.3 3.3 fusion.5
  382.8 3.8 multiply_reduce_fusion.27
  387.9 4.2 fusion.7
  392.1 100.0 %psum.7 = f32[64,192]{1,0:T(8,128)S(1)} all-reduce(f32[64,192]{1,0:T(8,128)} %fusion.7), channel_id=1, replica_groups=mesh['gx'=32,'yz'=16] {'gx','yz'}, use_global_device_ids=true, to_apply=%region_37.38 | all-reduce | flops 12288 | bytes 98304 | tf_op jit(solution)/shard_map/psum | solution.py:98
  493.3 4.7 fusion.6
  498.1 104.9 %while.52 = (s32[]{:T(128)}, f32[8,26,2,3,3,128]{5,0,4,3,2,1:T(8,128)S(1)}, s32[24]{0:T(128)S(1)}, f32[24,2,2,3,3,128]{5,1,4,3,2,0:T(2,128)}, f32[24,8,2,2,3,3,1...) while((s32[]{:T(128)}, f32[8,26,2,3,3,128]{5,0,4,3,2,1:T(8,128)S(1)}, s32[24]{0:T(128)S(1)}, ...), condition=%wide.region_34.35_spmd, body=%wide.region_25.34_spmd.sunk | while | flops 891653 | bytes 3411083 | solution.py:85
  604.4 2.9 rev.3
  607.3 161.5 %while.53 = (s32[]{:T(128)}, f32[8,2,2,3,3,128]{5,4,3,2,1,0:T(4,128)S(1)}, f32[12,8,2,2,3,3,128]{6,1,5,4,3,2,0:T(8,128)}, s32[]{:T(128)}) while((s32[]{:T(128)}, f32[8,2,2,3,3,128]{5,4,3,2,1,0:T(4,128)S(1)}, f32[12,8,2,2,3,3,128]{6,1,5,4,3,2,0:T(8,128)}, s32[]{:T(128)}) %tuple.163), condition=%wide.region_36.37_spmd, body=%wide.region_35.36_spmd.sunk | while | flops 36866 | bytes 1327209 | solution.py:94
  607.3 2.1 collective-permute-start.2
  610.3 12.3 %collective-permute-done.2 = f32[8,2,2,3,3,128]{5,4,3,2,1,0:T(4,128)S(1)} collective-permute-done((f32[8,2,2,3,3,128]{5,4,3,2,1,0:T(4,128)S(1)}, f32[8,2,2,3,3,128]{5,4,3,2,1,0:T(4,128)S(1)}, u32[]{:S(2)}, u32[]{:S(2)}) %collective-permute-start.2) | collective-permute-done | bytes 147488 | tf_op jit(solution)/shard_map/while/body/eval_jaxpr/ppermute | solution.py:12
  625.5 12.2 %collective-permute-done.2 = f32[8,2,2,3,3,128]{5,4,3,2,1,0:T(4,128)S(1)} collective-permute-done((f32[8,2,2,3,3,128]{5,4,3,2,1,0:T(4,128)S(1)}, f32[8,2,2,3,3,128]{5,4,3,2,1,0:T(4,128)S(1)}, u32[]{:S(2)}, u32[]{:S(2)}) %collective-permute-start.2) | collective-permute-done | bytes 147488 | tf_op jit(solution)/shard_map/while/body/eval_jaxpr/ppermute | solution.py:12
  640.7 10.2 %collective-permute-done.2 = f32[8,2,2,3,3,128]{5,4,3,2,1,0:T(4,128)S(1)} collective-permute-done((f32[8,2,2,3,3,128]{5,4,3,2,1,0:T(4,128)S(1)}, f32[8,2,2,3,3,128]{5,4,3,2,1,0:T(4,128)S(1)}, u32[]{:S(2)}, u32[]{:S(2)}) %collective-permute-start.2) | collective-permute-done | bytes 147488 | tf_op jit(solution)/shard_map/while/body/eval_jaxpr/ppermute | solution.py:12
  651.1 1.9 collective-permute-start.2
  653.9 10.2 %collective-permute-done.2 = f32[8,2,2,3,3,128]{5,4,3,2,1,0:T(4,128)S(1)} collective-permute-done((f32[8,2,2,3,3,128]{5,4,3,2,1,0:T(4,128)S(1)}, f32[8,2,2,3,3,128]{5,4,3,2,1,0:T(4,128)S(1)}, u32[]{:S(2)}, u32[]{:S(2)}) %collective-permute-start.2) | collective-permute-done | bytes 147488 | tf_op jit(solution)/shard_map/while/body/eval_jaxpr/ppermute | solution.py:12
  667.0 10.1 %collective-permute-done.2 = f32[8,2,2,3,3,128]{5,4,3,2,1,0:T(4,128)S(1)} collective-permute-done((f32[8,2,2,3,3,128]{5,4,3,2,1,0:T(4,128)S(1)}, f32[8,2,2,3,3,128]{5,4,3,2,1,0:T(4,128)S(1)}, u32[]{:S(2)}, u32[]{:S(2)}) %collective-permute-start.2) | collective-permute-done | bytes 147488 | tf_op jit(solution)/shard_map/while/body/eval_jaxpr/ppermute | solution.py:12
  677.2 1.9 collective-permute-start.2
  680.1 10.1 %collective-permute-done.2 = f32[8,2,2,3,3,128]{5,4,3,2,1,0:T(4,128)S(1)} collective-permute-done((f32[8,2,2,3,3,128]{5,4,3,2,1,0:T(4,128)S(1)}, f32[8,2,2,3,3,128]{5,4,3,2,1,0:T(4,128)S(1)}, u32[]{:S(2)}, u32[]{:S(2)}) %collective-permute-start.2) | collective-permute-done | bytes 147488 | tf_op jit(solution)/shard_map/while/body/eval_jaxpr/ppermute | solution.py:12
  693.2 10.1 %collective-permute-done.2 = f32[8,2,2,3,3,128]{5,4,3,2,1,0:T(4,128)S(1)} collective-permute-done((f32[8,2,2,3,3,128]{5,4,3,2,1,0:T(4,128)S(1)}, f32[8,2,2,3,3,128]{5,4,3,2,1,0:T(4,128)S(1)}, u32[]{:S(2)}, u32[]{:S(2)}) %collective-permute-start.2) | collective-permute-done | bytes 147488 | tf_op jit(solution)/shard_map/while/body/eval_jaxpr/ppermute | solution.py:12
  706.3 10.1 %collective-permute-done.2 = f32[8,2,2,3,3,128]{5,4,3,2,1,0:T(4,128)S(1)} collective-permute-done((f32[8,2,2,3,3,128]{5,4,3,2,1,0:T(4,128)S(1)}, f32[8,2,2,3,3,128]{5,4,3,2,1,0:T(4,128)S(1)}, u32[]{:S(2)}, u32[]{:S(2)}) %collective-permute-start.2) | collective-permute-done | bytes 147488 | tf_op jit(solution)/shard_map/while/body/eval_jaxpr/ppermute | solution.py:12
  719.4 10.1 %collective-permute-done.2 = f32[8,2,2,3,3,128]{5,4,3,2,1,0:T(4,128)S(1)} collective-permute-done((f32[8,2,2,3,3,128]{5,4,3,2,1,0:T(4,128)S(1)}, f32[8,2,2,3,3,128]{5,4,3,2,1,0:T(4,128)S(1)}, u32[]{:S(2)}, u32[]{:S(2)}) %collective-permute-start.2) | collective-permute-done | bytes 147488 | tf_op jit(solution)/shard_map/while/body/eval_jaxpr/ppermute | solution.py:12
  729.6 1.9 collective-permute-start.2
  732.5 10.1 %collective-permute-done.2 = f32[8,2,2,3,3,128]{5,4,3,2,1,0:T(4,128)S(1)} collective-permute-done((f32[8,2,2,3,3,128]{5,4,3,2,1,0:T(4,128)S(1)}, f32[8,2,2,3,3,128]{5,4,3,2,1,0:T(4,128)S(1)}, u32[]{:S(2)}, u32[]{:S(2)}) %collective-permute-start.2) | collective-permute-done | bytes 147488 | tf_op jit(solution)/shard_map/while/body/eval_jaxpr/ppermute | solution.py:12
  745.6 10.1 %collective-permute-done.2 = f32[8,2,2,3,3,128]{5,4,3,2,1,0:T(4,128)S(1)} collective-permute-done((f32[8,2,2,3,3,128]{5,4,3,2,1,0:T(4,128)S(1)}, f32[8,2,2,3,3,128]{5,4,3,2,1,0:T(4,128)S(1)}, u32[]{:S(2)}, u32[]{:S(2)}) %collective-permute-start.2) | collective-permute-done | bytes 147488 | tf_op jit(solution)/shard_map/while/body/eval_jaxpr/ppermute | solution.py:12
  758.7 10.1 %collective-permute-done.2 = f32[8,2,2,3,3,128]{5,4,3,2,1,0:T(4,128)S(1)} collective-permute-done((f32[8,2,2,3,3,128]{5,4,3,2,1,0:T(4,128)S(1)}, f32[8,2,2,3,3,128]{5,4,3,2,1,0:T(4,128)S(1)}, u32[]{:S(2)}, u32[]{:S(2)}) %collective-permute-start.2) | collective-permute-done | bytes 147488 | tf_op jit(solution)/shard_map/while/body/eval_jaxpr/ppermute | solution.py:12
  (1181 shorter events, 234.8 us)
Async XLA Ops:
  1.6 184.5 %copy-start.11 = (f32[2,2,3,3,128]{4,1,3,2,0:T(2,128)S(1)}, f32[2,2,3,3,128]{4,1,3,2,0:T(2,128)}, u32[]{:S(2)}) copy-start(f32[2,2,3,3,128]{4,1,3,2,0:T(2,128)} %param.12) | copy-start | bytes 55300
  2.4 18.2 %collective-permute-start = (f32[2,2,3,3,128]{4,1,3,2,0:T(2,128)S(1)}, f32[2,2,3,3,128]{4,1,3,2,0:T(2,128)S(1)}, u32[]{:S(2)}, u32[]{:S(2)}) collective-permute-start(f32[2,2,3,3,128]{4,1,3,2,0:T(2,128)S(1)} %get-tuple-element.507), channel_id=1, source_target_pairs={{16,0},{32,16},{48,32},{64,48},{80,64},{96,80},{112,96},{128,112},... | collective-permute-start | bytes 55304 | tf_op jit(solution)/shard_map/while/body/eval_jaxpr/ppermute | solution.py:12
  18.0 6.8 collective-permute-start.1
  24.9 11.7 %collective-permute-start = (f32[2,2,3,3,128]{4,1,3,2,0:T(2,128)S(1)}, f32[2,2,3,3,128]{4,1,3,2,0:T(2,128)S(1)}, u32[]{:S(2)}, u32[]{:S(2)}) collective-permute-start(f32[2,2,3,3,128]{4,1,3,2,0:T(2,128)S(1)} %get-tuple-element.507), channel_id=1, source_target_pairs={{16,0},{32,16},{48,32},{64,48},{80,64},{96,80},{112,96},{128,112},... | collective-permute-start | bytes 55304 | tf_op jit(solution)/shard_map/while/body/eval_jaxpr/ppermute | solution.py:12
  34.7 5.9 collective-permute-start.1
  40.8 11.8 %collective-permute-start = (f32[2,2,3,3,128]{4,1,3,2,0:T(2,128)S(1)}, f32[2,2,3,3,128]{4,1,3,2,0:T(2,128)S(1)}, u32[]{:S(2)}, u32[]{:S(2)}) collective-permute-start(f32[2,2,3,3,128]{4,1,3,2,0:T(2,128)S(1)} %get-tuple-element.507), channel_id=1, source_target_pairs={{16,0},{32,16},{48,32},{64,48},{80,64},{96,80},{112,96},{128,112},... | collective-permute-start | bytes 55304 | tf_op jit(solution)/shard_map/while/body/eval_jaxpr/ppermute | solution.py:12
  50.6 4.7 collective-permute-start.1
  55.4 11.8 %collective-permute-start = (f32[2,2,3,3,128]{4,1,3,2,0:T(2,128)S(1)}, f32[2,2,3,3,128]{4,1,3,2,0:T(2,128)S(1)}, u32[]{:S(2)}, u32[]{:S(2)}) collective-permute-start(f32[2,2,3,3,128]{4,1,3,2,0:T(2,128)S(1)} %get-tuple-element.507), channel_id=1, source_target_pairs={{16,0},{32,16},{48,32},{64,48},{80,64},{96,80},{112,96},{128,112},... | collective-permute-start | bytes 55304 | tf_op jit(solution)/shard_map/while/body/eval_jaxpr/ppermute | solution.py:12
  65.2 4.6 collective-permute-start.1
  69.9 11.8 %collective-permute-start = (f32[2,2,3,3,128]{4,1,3,2,0:T(2,128)S(1)}, f32[2,2,3,3,128]{4,1,3,2,0:T(2,128)S(1)}, u32[]{:S(2)}, u32[]{:S(2)}) collective-permute-start(f32[2,2,3,3,128]{4,1,3,2,0:T(2,128)S(1)} %get-tuple-element.507), channel_id=1, source_target_pairs={{16,0},{32,16},{48,32},{64,48},{80,64},{96,80},{112,96},{128,112},... | collective-permute-start | bytes 55304 | tf_op jit(solution)/shard_map/while/body/eval_jaxpr/ppermute | solution.py:12
  79.8 4.6 collective-permute-start.1
  84.4 11.8 %collective-permute-start = (f32[2,2,3,3,128]{4,1,3,2,0:T(2,128)S(1)}, f32[2,2,3,3,128]{4,1,3,2,0:T(2,128)S(1)}, u32[]{:S(2)}, u32[]{:S(2)}) collective-permute-start(f32[2,2,3,3,128]{4,1,3,2,0:T(2,128)S(1)} %get-tuple-element.507), channel_id=1, source_target_pairs={{16,0},{32,16},{48,32},{64,48},{80,64},{96,80},{112,96},{128,112},... | collective-permute-start | bytes 55304 | tf_op jit(solution)/shard_map/while/body/eval_jaxpr/ppermute | solution.py:12
  94.3 4.6 collective-permute-start.1
  99.0 11.8 %collective-permute-start = (f32[2,2,3,3,128]{4,1,3,2,0:T(2,128)S(1)}, f32[2,2,3,3,128]{4,1,3,2,0:T(2,128)S(1)}, u32[]{:S(2)}, u32[]{:S(2)}) collective-permute-start(f32[2,2,3,3,128]{4,1,3,2,0:T(2,128)S(1)} %get-tuple-element.507), channel_id=1, source_target_pairs={{16,0},{32,16},{48,32},{64,48},{80,64},{96,80},{112,96},{128,112},... | collective-permute-start | bytes 55304 | tf_op jit(solution)/shard_map/while/body/eval_jaxpr/ppermute | solution.py:12
  108.8 4.6 collective-permute-start.1
  113.5 11.8 %collective-permute-start = (f32[2,2,3,3,128]{4,1,3,2,0:T(2,128)S(1)}, f32[2,2,3,3,128]{4,1,3,2,0:T(2,128)S(1)}, u32[]{:S(2)}, u32[]{:S(2)}) collective-permute-start(f32[2,2,3,3,128]{4,1,3,2,0:T(2,128)S(1)} %get-tuple-element.507), channel_id=1, source_target_pairs={{16,0},{32,16},{48,32},{64,48},{80,64},{96,80},{112,96},{128,112},... | collective-permute-start | bytes 55304 | tf_op jit(solution)/shard_map/while/body/eval_jaxpr/ppermute | solution.py:12
  123.3 4.6 collective-permute-start.1
  128.0 11.8 %collective-permute-start = (f32[2,2,3,3,128]{4,1,3,2,0:T(2,128)S(1)}, f32[2,2,3,3,128]{4,1,3,2,0:T(2,128)S(1)}, u32[]{:S(2)}, u32[]{:S(2)}) collective-permute-start(f32[2,2,3,3,128]{4,1,3,2,0:T(2,128)S(1)} %get-tuple-element.507), channel_id=1, source_target_pairs={{16,0},{32,16},{48,32},{64,48},{80,64},{96,80},{112,96},{128,112},... | collective-permute-start | bytes 55304 | tf_op jit(solution)/shard_map/while/body/eval_jaxpr/ppermute | solution.py:12
  137.8 4.6 collective-permute-start.1
  142.5 11.8 %collective-permute-start = (f32[2,2,3,3,128]{4,1,3,2,0:T(2,128)S(1)}, f32[2,2,3,3,128]{4,1,3,2,0:T(2,128)S(1)}, u32[]{:S(2)}, u32[]{:S(2)}) collective-permute-start(f32[2,2,3,3,128]{4,1,3,2,0:T(2,128)S(1)} %get-tuple-element.507), channel_id=1, source_target_pairs={{16,0},{32,16},{48,32},{64,48},{80,64},{96,80},{112,96},{128,112},... | collective-permute-start | bytes 55304 | tf_op jit(solution)/shard_map/while/body/eval_jaxpr/ppermute | solution.py:12
  152.3 4.6 collective-permute-start.1
  157.0 11.8 %collective-permute-start = (f32[2,2,3,3,128]{4,1,3,2,0:T(2,128)S(1)}, f32[2,2,3,3,128]{4,1,3,2,0:T(2,128)S(1)}, u32[]{:S(2)}, u32[]{:S(2)}) collective-permute-start(f32[2,2,3,3,128]{4,1,3,2,0:T(2,128)S(1)} %get-tuple-element.507), channel_id=1, source_target_pairs={{16,0},{32,16},{48,32},{64,48},{80,64},{96,80},{112,96},{128,112},... | collective-permute-start | bytes 55304 | tf_op jit(solution)/shard_map/while/body/eval_jaxpr/ppermute | solution.py:12
  166.9 4.6 collective-permute-start.1
  171.6 11.8 %collective-permute-start = (f32[2,2,3,3,128]{4,1,3,2,0:T(2,128)S(1)}, f32[2,2,3,3,128]{4,1,3,2,0:T(2,128)S(1)}, u32[]{:S(2)}, u32[]{:S(2)}) collective-permute-start(f32[2,2,3,3,128]{4,1,3,2,0:T(2,128)S(1)} %get-tuple-element.507), channel_id=1, source_target_pairs={{16,0},{32,16},{48,32},{64,48},{80,64},{96,80},{112,96},{128,112},... | collective-permute-start | bytes 55304 | tf_op jit(solution)/shard_map/while/body/eval_jaxpr/ppermute | solution.py:12
  181.4 4.6 collective-permute-start.1
  192.5 2.7 copy-start.3
  200.2 2.7 copy-start.3
  207.9 2.7 copy-start.3
  215.6 2.7 copy-start.3
  223.2 2.7 copy-start.3
  230.9 2.7 copy-start.3
  238.6 2.7 copy-start.3
  246.3 2.7 copy-start.3
  254.0 2.7 copy-start.3
  261.7 2.7 copy-start.3
  269.4 2.7 copy-start.3
  277.1 2.7 copy-start.3
  284.8 2.7 copy-start.3
  292.4 2.7 copy-start.3
  300.1 2.7 copy-start.3
  307.8 2.7 copy-start.3
  315.5 2.7 copy-start.3
  323.2 2.7 copy-start.3
  330.9 2.7 copy-start.3
  338.6 2.7 copy-start.3
  346.3 2.7 copy-start.3
  353.9 2.7 copy-start.3
  392.1 101.2 %copy-start.1 = (f32[8,8,2,2,3,3,128]{6,1,5,4,3,2,0:T(8,128)S(1)}, f32[8,8,2,2,3,3,128]{6,1,5,4,3,2,0:T(8,128)}, u32[]{:S(2)}) copy-start(f32[8,8,2,2,3,3,128]{6,1,5,4,3,2,0:T(8,128)} %copy-done) | copy-start | bytes 3538948
  392.1 101.2 %copy-start.9 = (f32[64,192]{1,0:T(8,128)S(1)}, f32[64,192]{1,0:T(8,128)}, u32[]{:S(2)}) copy-start(f32[64,192]{1,0:T(8,128)} %reshape.184) | copy-start | bytes 147460
  604.4 164.5 %copy-start.6 = (f32[8,8,2,3,3,128]{5,1,4,3,2,0:T(8,128)S(1)}, f32[8,8,2,3,3,128]{5,1,4,3,2,0:T(8,128)}, u32[]{:S(2)}) copy-start(f32[8,8,2,3,3,128]{5,1,4,3,2,0:T(8,128)} %get-tuple-element.198) | copy-start | bytes 1769476
  607.2 161.6 %copy-start.5 = (f32[8,8,2,3,3,128]{5,1,4,3,2,0:T(8,128)S(1)}, f32[8,8,2,3,3,128]{5,1,4,3,2,0:T(8,128)}, u32[]{:S(2)}) copy-start(f32[8,8,2,3,3,128]{5,1,4,3,2,0:T(8,128)} %get-tuple-element.197) | copy-start | bytes 1769476
  607.3 161.6 %copy-start.4 = (f32[8,8,2,3,3,128]{5,1,4,3,2,0:T(8,128)S(1)}, f32[8,8,2,3,3,128]{5,1,4,3,2,0:T(8,128)}, u32[]{:S(2)}) copy-start(f32[8,8,2,3,3,128]{5,1,4,3,2,0:T(8,128)} %get-tuple-element.196) | copy-start | bytes 1769476
  607.3 15.2 %collective-permute-start.2 = (f32[8,2,2,3,3,128]{5,4,3,2,1,0:T(4,128)S(1)}, f32[8,2,2,3,3,128]{5,4,3,2,1,0:T(4,128)S(1)}, u32[]{:S(2)}, u32[]{:S(2)}) collective-permute-start(f32[8,2,2,3,3,128]{5,4,3,2,1,0:T(4,128)S(1)} %get-tuple-element.580), channel_id=1, source_target_pairs={{496,0},{0,16},{16,32},{32,48},{48,64},{64,80},{80,96},{96,112},{1... | collective-permute-start | bytes 442376 | tf_op jit(solution)/shard_map/while/body/eval_jaxpr/ppermute | solution.py:12
  622.7 15.1 %collective-permute-start.2 = (f32[8,2,2,3,3,128]{5,4,3,2,1,0:T(4,128)S(1)}, f32[8,2,2,3,3,128]{5,4,3,2,1,0:T(4,128)S(1)}, u32[]{:S(2)}, u32[]{:S(2)}) collective-permute-start(f32[8,2,2,3,3,128]{5,4,3,2,1,0:T(4,128)S(1)} %get-tuple-element.580), channel_id=1, source_target_pairs={{496,0},{0,16},{16,32},{32,48},{48,64},{64,80},{80,96},{96,112},{1... | collective-permute-start | bytes 442376 | tf_op jit(solution)/shard_map/while/body/eval_jaxpr/ppermute | solution.py:12
  637.9 13.1 %collective-permute-start.2 = (f32[8,2,2,3,3,128]{5,4,3,2,1,0:T(4,128)S(1)}, f32[8,2,2,3,3,128]{5,4,3,2,1,0:T(4,128)S(1)}, u32[]{:S(2)}, u32[]{:S(2)}) collective-permute-start(f32[8,2,2,3,3,128]{5,4,3,2,1,0:T(4,128)S(1)} %get-tuple-element.580), channel_id=1, source_target_pairs={{496,0},{0,16},{16,32},{32,48},{48,64},{64,80},{80,96},{96,112},{1... | collective-permute-start | bytes 442376 | tf_op jit(solution)/shard_map/while/body/eval_jaxpr/ppermute | solution.py:12
  651.1 13.0 %collective-permute-start.2 = (f32[8,2,2,3,3,128]{5,4,3,2,1,0:T(4,128)S(1)}, f32[8,2,2,3,3,128]{5,4,3,2,1,0:T(4,128)S(1)}, u32[]{:S(2)}, u32[]{:S(2)}) collective-permute-start(f32[8,2,2,3,3,128]{5,4,3,2,1,0:T(4,128)S(1)} %get-tuple-element.580), channel_id=1, source_target_pairs={{496,0},{0,16},{16,32},{32,48},{48,64},{64,80},{80,96},{96,112},{1... | collective-permute-start | bytes 442376 | tf_op jit(solution)/shard_map/while/body/eval_jaxpr/ppermute | solution.py:12
  664.2 13.0 %collective-permute-start.2 = (f32[8,2,2,3,3,128]{5,4,3,2,1,0:T(4,128)S(1)}, f32[8,2,2,3,3,128]{5,4,3,2,1,0:T(4,128)S(1)}, u32[]{:S(2)}, u32[]{:S(2)}) collective-permute-start(f32[8,2,2,3,3,128]{5,4,3,2,1,0:T(4,128)S(1)} %get-tuple-element.580), channel_id=1, source_target_pairs={{496,0},{0,16},{16,32},{32,48},{48,64},{64,80},{80,96},{96,112},{1... | collective-permute-start | bytes 442376 | tf_op jit(solution)/shard_map/while/body/eval_jaxpr/ppermute | solution.py:12
  677.2 13.0 %collective-permute-start.2 = (f32[8,2,2,3,3,128]{5,4,3,2,1,0:T(4,128)S(1)}, f32[8,2,2,3,3,128]{5,4,3,2,1,0:T(4,128)S(1)}, u32[]{:S(2)}, u32[]{:S(2)}) collective-permute-start(f32[8,2,2,3,3,128]{5,4,3,2,1,0:T(4,128)S(1)} %get-tuple-element.580), channel_id=1, source_target_pairs={{496,0},{0,16},{16,32},{32,48},{48,64},{64,80},{80,96},{96,112},{1... | collective-permute-start | bytes 442376 | tf_op jit(solution)/shard_map/while/body/eval_jaxpr/ppermute | solution.py:12
  690.3 13.0 %collective-permute-start.2 = (f32[8,2,2,3,3,128]{5,4,3,2,1,0:T(4,128)S(1)}, f32[8,2,2,3,3,128]{5,4,3,2,1,0:T(4,128)S(1)}, u32[]{:S(2)}, u32[]{:S(2)}) collective-permute-start(f32[8,2,2,3,3,128]{5,4,3,2,1,0:T(4,128)S(1)} %get-tuple-element.580), channel_id=1, source_target_pairs={{496,0},{0,16},{16,32},{32,48},{48,64},{64,80},{80,96},{96,112},{1... | collective-permute-start | bytes 442376 | tf_op jit(solution)/shard_map/while/body/eval_jaxpr/ppermute | solution.py:12
  703.4 13.0 %collective-permute-start.2 = (f32[8,2,2,3,3,128]{5,4,3,2,1,0:T(4,128)S(1)}, f32[8,2,2,3,3,128]{5,4,3,2,1,0:T(4,128)S(1)}, u32[]{:S(2)}, u32[]{:S(2)}) collective-permute-start(f32[8,2,2,3,3,128]{5,4,3,2,1,0:T(4,128)S(1)} %get-tuple-element.580), channel_id=1, source_target_pairs={{496,0},{0,16},{16,32},{32,48},{48,64},{64,80},{80,96},{96,112},{1... | collective-permute-start | bytes 442376 | tf_op jit(solution)/shard_map/while/body/eval_jaxpr/ppermute | solution.py:12
  716.5 13.0 %collective-permute-start.2 = (f32[8,2,2,3,3,128]{5,4,3,2,1,0:T(4,128)S(1)}, f32[8,2,2,3,3,128]{5,4,3,2,1,0:T(4,128)S(1)}, u32[]{:S(2)}, u32[]{:S(2)}) collective-permute-start(f32[8,2,2,3,3,128]{5,4,3,2,1,0:T(4,128)S(1)} %get-tuple-element.580), channel_id=1, source_target_pairs={{496,0},{0,16},{16,32},{32,48},{48,64},{64,80},{80,96},{96,112},{1... | collective-permute-start | bytes 442376 | tf_op jit(solution)/shard_map/while/body/eval_jaxpr/ppermute | solution.py:12
  729.6 13.0 %collective-permute-start.2 = (f32[8,2,2,3,3,128]{5,4,3,2,1,0:T(4,128)S(1)}, f32[8,2,2,3,3,128]{5,4,3,2,1,0:T(4,128)S(1)}, u32[]{:S(2)}, u32[]{:S(2)}) collective-permute-start(f32[8,2,2,3,3,128]{5,4,3,2,1,0:T(4,128)S(1)} %get-tuple-element.580), channel_id=1, source_target_pairs={{496,0},{0,16},{16,32},{32,48},{48,64},{64,80},{80,96},{96,112},{1... | collective-permute-start | bytes 442376 | tf_op jit(solution)/shard_map/while/body/eval_jaxpr/ppermute | solution.py:12
  742.7 13.0 %collective-permute-start.2 = (f32[8,2,2,3,3,128]{5,4,3,2,1,0:T(4,128)S(1)}, f32[8,2,2,3,3,128]{5,4,3,2,1,0:T(4,128)S(1)}, u32[]{:S(2)}, u32[]{:S(2)}) collective-permute-start(f32[8,2,2,3,3,128]{5,4,3,2,1,0:T(4,128)S(1)} %get-tuple-element.580), channel_id=1, source_target_pairs={{496,0},{0,16},{16,32},{32,48},{48,64},{64,80},{80,96},{96,112},{1... | collective-permute-start | bytes 442376 | tf_op jit(solution)/shard_map/while/body/eval_jaxpr/ppermute | solution.py:12
  755.8 13.0 %collective-permute-start.2 = (f32[8,2,2,3,3,128]{5,4,3,2,1,0:T(4,128)S(1)}, f32[8,2,2,3,3,128]{5,4,3,2,1,0:T(4,128)S(1)}, u32[]{:S(2)}, u32[]{:S(2)}) collective-permute-start(f32[8,2,2,3,3,128]{5,4,3,2,1,0:T(4,128)S(1)} %get-tuple-element.580), channel_id=1, source_target_pairs={{496,0},{0,16},{16,32},{32,48},{48,64},{64,80},{80,96},{96,112},{1... | collective-permute-start | bytes 442376 | tf_op jit(solution)/shard_map/while/body/eval_jaxpr/ppermute | solution.py:12
  (7 other events, 9.9 us)
where the time goes:
time: 780 us; the launch traced here: 771 us
  local copies, waits for them, and re-layouts  177 us (23%)
  starting transfers between devices  171 us (22%)
  waiting for transfers between devices  160 us (21%)
  blocking collectives  100 us (13%)
  loops' own time  96.8 us (12%)
  other arithmetic  53.1 us (7%)
  matrix products  12.2 us (2%)
    ppermute x36, starting transfers between devices, from_behind(): return lax.ppermute(block, axis, route)  171 us
    ppermute x36, waiting for transfers between devices, from_behind(): return lax.ppermute(block, axis, route)  160 us
    psum x1, blocking collectives, per_device(): summed = lax.psum(partial_grad, ('gx', 'yz'))  100 us
    mul x364, local copies, waits for them, and re-layouts, matmul_three(): left[..., :, :, None, :] * right[..., None, :, :, :]  64.4 us
    another operation x1, loops' own time, per_device(): lax.scan(forward_step, gauge_links, offsets)  51.7 us
    another operation x1, loops' own time, per_device(): lax.scan(backward_step, accumulator, (offsets, line_grad, all_lines))  44 us
    dynamic_slice x48, local copies, waits for them, and re-layouts, per_device(): lax.scan(forward_step, gauge_links, offsets)  29.5 us
    squeeze x24, local copies, waits for them, and re-layouts, per_device(): lax.scan(backward_step, accumulator, (offsets, line_grad, all_lines))  22.2 us
  transfers between devices with their start and end apart: 36, of which 24 were waited for; matrix products, arithmetic and copies ran while one was open for 1% of the time, Pallas kernels for 0%

commit v1 on v0

v1 whole, which is shorter than its diff:
```python
import functools
import math

import jax
import jax.numpy as jnp
from jax import lax
from jax.experimental import pallas as pl
from jax.experimental.pallas import tpu as pltpu
from jax.sharding import PartitionSpec as P

C = 8
HALF = 320
HIGHEST = lax.Precision.HIGHEST


def comp(ri, a, b):
    return (ri * 3 + a) * 3 + b


def product(left, right, dag_left=False, dag_right=False):
    result = [None] * 18
    for a in range(3):
        for b in range(3):
            real = imag = None
            for k in range(3):
                l_at = (k, a) if dag_left else (a, k)
                r_at = (b, k) if dag_right else (k, b)
                l_re, l_im = left[comp(0, *l_at)], left[comp(1, *l_at)]
                r_re, r_im = right[comp(0, *r_at)], right[comp(1, *r_at)]
                rr, ii = l_re * r_re, l_im * r_im
                ri, ir = l_re * r_im, l_im * r_re
                term_re = rr + ii if dag_left != dag_right else rr - ii
                if not dag_left and not dag_right:
                    term_im = ri + ir
                elif dag_left and not dag_right:
                    term_im = ri - ir
                elif dag_right and not dag_left:
                    term_im = ir - ri
                else:
                    term_im = -(ri + ir)
                real = term_re if real is None else real + term_re
                imag = term_im if imag is None else imag + term_im
            result[comp(0, a, b)] = real
            result[comp(1, a, b)] = imag
    return result


def pack_kernel(links, field, cot, out, rows):
    rows[...] = jnp.zeros_like(rows)
    for x in range(2):
        base = x * HALF
        for ri in range(2):
            for a in range(3):
                first = comp(ri, a, 0)
                rows[pl.ds(base + 288 + first, 3), :] = links[x, ri, a]
                for c in range(C):
                    rows[pl.ds(base + first * 8 + c, 3, stride=8), :] = field[c, x, ri, a]
                    rows[pl.ds(base + 144 + first * 8 + c, 3, stride=8), :] = cot[c, x, ri, a]
    for block in range(5):
        turned = rows[pl.ds(128 * block, 128), :].T
        out[:, :, pl.ds(128 * block, 128)] = turned.reshape(32, 4, 128)


def layer_kernel(lines, packed, weights, grad_out, gw_out, rows, frame, wt, wp, gt, pair, windows, mixed, back, acc):
    shape = (C, 128)
    lane = lax.broadcasted_iota(jnp.int32, shape, 1)
    for block in range(5):
        turned = packed[:, :, pl.ds(128 * block, 128)].reshape(128, 128)
        rows[pl.ds(128 * block, 128), :] = turned.T

    def load8(x, offset):
        return [rows[pl.ds(x * HALF + offset + 8 * k, 8), :] for k in range(18)]

    def load_link(x):
        return [jnp.broadcast_to(rows[pl.ds(x * HALF + 288 + k, 1), :], shape) for k in range(18)]

    one = [jnp.full(shape, 1.0 if k in (0, 4, 8) else 0.0, jnp.float32) for k in range(18)]
    even = load_link(0)
    scan = product(even, load_link(1))
    step = 1
    while step < 32:
        moved = [pltpu.roll(v, 4 * step, 1) for v in scan]
        longer = product(moved, scan)
        scan = [jnp.where(lane >= 4 * step, n, v) for n, v in zip(longer, scan)]
        step *= 2
    for k in range(18):
        before = jnp.where(lane >= 4, pltpu.roll(scan[k], 4, 1), one[k])
        frame[0, k] = before
        whole = scan[k]
        reach = 1
        while reach < 32:
            whole = jnp.where(lane < 128 - 4 * reach, pltpu.roll(whole, 128 - 4 * reach, 1), whole)
            reach *= 2
        frame[2, k] = whole
    v_odd = product([frame[0, k] for k in range(18)], load_link(0))
    for k in range(18):
        frame[1, k] = v_odd[k]

    def get_frame(which):
        return [frame[which, k] for k in range(18)]

    for x in range(2):
        for offset, target in ((0, wt), (144, gt)):
            turned = product(product(get_frame(x), load8(x, offset)), get_frame(x), dag_right=True)
            for k in range(18):
                target[x, k] = turned[k]
        turned = product(product(get_frame(2), [wt[x, k] for k in range(18)]), get_frame(2), dag_right=True)
        for k in range(18):
            wp[x, k] = turned[k]

    for k in range(18):
        columns = pl.ds(128 * k, 128)
        for t in range(lines + 1):
            x, m = (t + 1) % 2, (t + 1) // 2
            value = wt[x, k]
            if m:
                value = pltpu.roll(jnp.where(lane < 4 * m, wp[x, k], value), 128 - 4 * m, 1)
            windows[pl.ds(8 * t, 8), columns] = value

    def spread(x, i):
        return [jnp.broadcast_to(gt[x, k, pl.ds(i, 1), :], shape) for k in range(18)]

    for x in range(2):
        @pl.loop(0, C)
        def _(i):
            value = product([wt[x, k] for k in range(18)], spread(x, i), dag_left=True)
            for k in range(18):
                pair[pl.ds(pl.multiple_of(64 * x + 8 * i, 8), 8), pl.ds(128 * k, 128)] = value[k]

    gw2 = lax.dot_general(pair[...], windows[...], (((1,), (1,)), ((), ())), precision=HIGHEST,
                          preferred_element_type=jnp.float32)
    width = lines * C
    gw_out[...] = gw2[:64, :width] + gw2[64:, 8:8 + width]

    mixed[...] = jnp.dot(weights[...], windows[...], precision=HIGHEST, preferred_element_type=jnp.float32)
    back[...] = lax.dot_general(weights[...], pair[...], (((0,), (0,)), ((), ())), precision=HIGHEST,
                                preferred_element_type=jnp.float32)

    for k in range(18):
        columns = pl.ds(128 * k, 128)
        for x in range(2):
            inside = jnp.zeros(shape, jnp.float32)
            wrapped = jnp.zeros(shape, jnp.float32)
            for t in range(lines + 1):
                if (t + 1) % 2 != x:
                    continue
                m = (t + 1) // 2
                value = back[pl.ds(8 * t, 8), columns]
                if m:
                    value = pltpu.roll(value, 4 * m, 1)
                    wrapped = wrapped + jnp.where(lane < 4 * m, value, 0.0)
                    inside = inside + jnp.where(lane < 4 * m, 0.0, value)
                else:
                    inside = inside + value
            acc[x, k] = inside
            wp[x, k] = wrapped

    for x in range(2):
        turned = product(product(get_frame(2), [wp[x, k] for k in range(18)], dag_left=True), get_frame(2))
        for k in range(18):
            acc[x, k] = acc[x, k] + turned[k]

        @pl.loop(0, C)
        def _(i):
            here = [mixed[pl.ds(pl.multiple_of(64 * x + 8 * i, 8), 8), pl.ds(128 * k, 128)] for k in range(18)]
            value = product(spread(x, i), here, dag_right=True)
            for k in range(18):
                acc[x, k] = acc[x, k] + value[k]

        turned = product(product(get_frame(x), [acc[x, k] for k in range(18)], dag_left=True), get_frame(x))
        for k in range(18):
            rows[pl.ds(144 * x + 8 * k, 8), :] = turned[k]
    rows[pl.ds(288, 96), :] = jnp.zeros((96, 128), jnp.float32)
    for block in range(3):
        turned = rows[pl.ds(128 * block, 128), :].T
        grad_out[:, :, pl.ds(128 * block, 128)] = turned.reshape(32, 4, 128)


def unpack_kernel(packed, out, rows):
    for block in range(3):
        turned = packed[:, :, pl.ds(128 * block, 128)].reshape(128, 128)
        rows[pl.ds(128 * block, 128), :] = turned.T
    for x in range(2):
        for ri in range(2):
            for a in range(3):
                for c in range(C):
                    out[c, x, ri, a] = rows[pl.ds(144 * x + comp(ri, a, 0) * 8 + c, 3, stride=8), :]


def per_device(gauge_links, in_field, cotangent, bilinear_weights):
    lines = bilinear_weights.shape[2]
    width = lines * C
    f32 = jnp.float32
    n_gx, n_yz = lax.axis_size("gx"), lax.axis_size("yz")
    flat = bilinear_weights.reshape(C * C, width)
    weights = jnp.concatenate([jnp.pad(flat, ((0, 0), (0, 8))), jnp.pad(flat, ((0, 0), (8, 0)))], axis=0)
    vmem = lambda *shape: pltpu.VMEM(shape, f32)
    packed = pl.pallas_call(
        pack_kernel,
        out_shape=jax.ShapeDtypeStruct((32, 4, 640), f32),
        scratch_shapes=[vmem(640, 128)],
        name="pack",
    )(gauge_links, in_field, cotangent)
    packed = lax.all_to_all(packed, "gx", 0, 0, tiled=True)
    wide = 18 * 128
    grad_part, gw_part = pl.pallas_call(
        functools.partial(layer_kernel, lines),
        out_shape=(jax.ShapeDtypeStruct((32, 4, 384), f32), jax.ShapeDtypeStruct((64, width), f32)),
        scratch_shapes=[
            vmem(640, 128),
            vmem(3, 18, 8, 128),
            vmem(2, 18, 8, 128),
            vmem(2, 18, 8, 128),
            vmem(2, 18, 8, 128),
            vmem(128, wide),
            vmem(width + 8, wide),
            vmem(128, wide),
            vmem(width + 8, wide),
            vmem(2, 18, 8, 128),
        ],
        name="layer",
    )(packed, weights)
    gw_part = lax.all_to_all(gw_part.reshape(n_yz, 64 // n_yz, width), "yz", 0, 0, tiled=True)
    gw_part = jnp.sum(gw_part, axis=0)
    both = jnp.concatenate([grad_part[:, :, :288], jnp.broadcast_to(gw_part[None], (n_gx,) + gw_part.shape)], axis=2)
    both = lax.all_to_all(both, "gx", 0, 0, tiled=True)
    total = jnp.sum(both[:, :, 288:], axis=0)
    scale = 1.0 / math.sqrt(100.0 * 2 * n_gx * 128 * n_yz)
    total = jnp.broadcast_to((total * scale)[None], (n_yz,) + total.shape)
    grad_weights = lax.all_to_all(total, "yz", 0, 0, tiled=True).reshape(C, C, lines, C)
    back = jnp.pad(both[:, :, :288], ((0, 0), (0, 0), (0, 96)))
    grad_field = pl.pallas_call(
        unpack_kernel,
        out_shape=jax.ShapeDtypeStruct(in_field.shape, f32),
        scratch_shapes=[vmem(384, 128)],
        name="unpack",
    )(back)
    return (grad_field, grad_weights)


def solution(mesh):
    placed = (
        P("gx", None, None, None, "yz"),
        P(None, "gx", None, None, None, "yz"),
        P(None, "gx", None, None, None, "yz"),
        P(),
    )
    return jax.shard_map(
        per_device,
        mesh=mesh,
        in_specs=placed,
        out_specs=(P(None, "gx", None, None, None, "yz"), P()),
        check_vma=False,
    )
```

time: 780 us -> 97.1 us (0.12)
  the two profiles are of different devices: /device:TPU:2 before, /device:TPU:1 now
where the time goes in v1:
time: 97.1 us; the launch traced here: 96 us
  blocking collectives  33.4 us (34%)
  starting transfers between devices  22.5 us (23%)
  waiting for transfers between devices  15.6 us (16%)
  Pallas kernels  12.6 us (13%)
  local copies, waits for them, and re-layouts  9.44 us (10%)
  other arithmetic  1.77 us (2%)
    all_to_all x1, blocking collectives, per_device(): both = lax.all_to_all(both, 'gx', 0, 0, tiled=True)  18.9 us
    all_to_all x1, starting transfers between devices, per_device(): packed = lax.all_to_all(packed, 'gx', 0, 0, tiled=True)  17.4 us
    all_to_all x1, blocking collectives, per_device(): lax.all_to_all(gw_part.reshape(n_yz, 64 // n_yz, width), 'yz', 0, 0, tile...  14.5 us
    all_to_all x1, waiting for transfers between devices, per_device(): packed = lax.all_to_all(packed, 'gx', 0, 0, tiled=True)  12.7 us
    pallas_call x1, Pallas kernels, per_device(): pl.pallas_call(functools.partial(layer_kernel, lines), out_shape=(jax.Sha...  8.86 us
    unnamed x16, local copies, waits for them, and re-layouts  7.39 us
    all_to_all x1, starting transfers between devices, per_device(): lax.all_to_all(total, 'yz', 0, 0, tiled=True).reshape(C, C, lines, C)  5.14 us
    all_to_all x1, waiting for transfers between devices, per_device(): lax.all_to_all(total, 'yz', 0, 0, tiled=True).reshape(C, C, lines, C)  2.88 us
  transfers between devices with their start and end apart: 2, of which 2 were waited for; matrix products, arithmetic and copies ran while one was open for 4% of the time, Pallas kernels for 2%

profile of v1, /device:TPU:1, one launch (start us, length us, event | category | flops | bytes accessed | tf_op | source)
XLA Modules:
  0.0 96.0 jit_solution(11708407738980803014)
XLA Ops:
  0.6 1.3 %copy.11.links = f32[2,2,3,3,128]{4,3,2,1,0:T(4,128)} copy(f32[2,2,3,3,128]{4,1,3,2,0:T(2,128)} %param.4) | data formatting | bytes 36864 | tf_op args[0]
  2.0 0.0 copy-start.3
  2.0 1.7 %copy.12.field = f32[8,2,2,3,3,128]{5,4,3,2,1,0:T(4,128)} copy(f32[8,2,2,3,3,128]{5,2,4,3,1,0:T(2,128)} %param.5) | data formatting | bytes 294912 | tf_op args[1]
  3.6 0.0 copy-done.3
  3.6 0.7 copy.13.cot
  4.4 2.0 %pack.1 = f32[32,4,640]{2,1,0:T(4,128)} custom-call(f32[2,2,3,3,128]{4,3,2,1,0:T(4,128)} %copy.11.links, f32[8,2,2,3,3,128]{5,4,3,2,1,0:T(4,128)} %copy.12.field, f32[8,2,2,3,3,128]{5,4,3,2,1,0:T(4,128)} %copy.13.cot), custom_call_target="tpu_custom_call" | custom-call | tf_op jit(solution)/shard_map/pack/pallas_call | solution.py:198
  6.4 0.0 copy-start.1
  6.4 17.4 %all-to-all-start = ((f32[32,4,640]{2,1,0:T(4,128)}), f32[32,4,640]{2,1,0:T(4,128)S(1)}, u32[]{:S(2)}, u32[]{:S(2)}) async-start(f32[32,4,640]{2,1,0:T(4,128)} %pack.1), calls=%async_computation | async-start | bytes 655360 | tf_op jit(solution)/shard_map/all_to_all | solution.py:204
  23.7 0.0 copy-done.1
  23.7 0.3 copy.14
  24.0 0.3 reshape.17
  24.3 0.7 select_maximum_fusion.weights
  25.0 12.7 %all-to-all-done.packed = f32[32,4,640]{2,1,0:T(4,128)S(1)} async-done(((f32[32,4,640]{2,1,0:T(4,128)}), f32[32,4,640]{2,1,0:T(4,128)S(1)}, u32[]{:S(2)}, u32[]{:S(2)}) %all-to-all-start) | async-done | bytes 327712 | tf_op jit(solution)/shard_map/all_to_all | solution.py:204
  37.8 0.0 copy-start
  37.8 0.7 copy-done
  38.5 8.9 %layer.1 = (f32[32,4,384]{2,1,0:T(4,128)}, f32[64,192]{1,0:T(8,128)}) custom-call(f32[32,4,640]{2,1,0:T(4,128)} %copy-done, f32[128,200]{1,0:T(8,128)} %select_maximum_fusion.weights), custom_call_target="tpu_custom_call" | custom-call | tf_op jit(solution)/shard_map/layer/pallas_call | solution.py:206
  47.3 0.9 reshape.18
  48.2 0.0 copy-start.2
  48.2 14.5 %all_to_all.20 = f32[16,4,192]{2,1,0:T(4,128)S(1)} all-to-all(f32[16,4,192]{2,1,0:T(4,128)S(1)} %reshape.18), channel_id=1, replica_groups=mesh['gx'=32,'yz'=16] {'yz'}, dimensions={0} | all-to-all | bytes 98304 | tf_op jit(solution)/shard_map/all_to_all | solution.py:223
  62.8 0.0 copy-done.2
  62.8 0.1 pad_maximum_fusion
  63.0 18.9 %all_to_all.21 = f32[32,4,480]{2,1,0:T(4,128)S(1)} all-to-all(f32[32,4,480]{2,1,0:T(4,128)S(1)} %pad_maximum_fusion), channel_id=1, replica_groups=mesh['gx'=32,'yz'=16] {'gx'}, dimensions={0} | all-to-all | bytes 491520 | tf_op jit(solution)/shard_map/all_to_all | solution.py:226
  81.8 0.1 slice_reduce_fusion
  82.0 0.6 broadcast_in_dim.5
  82.6 0.0 copy-start.4
  82.6 5.1 %all-to-all-start.3 = ((f32[16,4,192]{2,1,0:T(4,128)}), f32[16,4,192]{2,1,0:T(4,128)S(1)}, u32[]{:S(2)}, u32[]{:S(2)}) async-start(f32[16,4,192]{2,1,0:T(4,128)} %broadcast_in_dim.5), calls=%async_computation.3 | async-start | bytes 131072 | tf_op jit(solution)/shard_map/all_to_all | solution.py:230
  87.8 0.0 copy-done.4
  87.8 0.7 slice_select_fusion.packed
  88.5 1.7 %unpack.1 = f32[8,2,2,3,3,128]{5,4,3,2,1,0:T(4,128)} custom-call(f32[32,4,384]{2,1,0:T(4,128)} %slice_select_fusion.packed), custom_call_target="tpu_custom_call" | custom-call | tf_op jit(solution)/shard_map/unpack/pallas_call | solution.py:232
  90.3 1.7 %copy.15 = f32[8,2,2,3,3,128]{5,2,4,3,1,0:T(2,128)} copy(f32[8,2,2,3,3,128]{5,4,3,2,1,0:T(4,128)} %unpack.1) | data formatting | bytes 294912
  91.9 2.9 %all-to-all-done.3 = f32[16,4,192]{2,1,0:T(4,128)S(1)} async-done(((f32[16,4,192]{2,1,0:T(4,128)}), f32[16,4,192]{2,1,0:T(4,128)S(1)}, u32[]{:S(2)}, u32[]{:S(2)}) %all-to-all-start.3) | async-done | bytes 49184 | tf_op jit(solution)/shard_map/all_to_all | solution.py:230
  94.8 0.3 reshape.19
  95.1 1.0 %copy.16 = f32[8,8,24,8]{2,3,1,0:T(8,128)} copy(f32[8,8,24,8]{3,2,1,0:T(8,128)S(1)} %reshape.19) | data formatting | bytes 98304
  (3 shorter events, 0.1 us)
Async XLA Ops:
  2.0 1.7 %copy-start.3 = (f32[8,2,2,3,3,128]{5,2,4,3,1,0:T(2,128)S(1)}, f32[8,2,2,3,3,128]{5,2,4,3,1,0:T(2,128)}, u32[]{:S(2)}) copy-start(f32[8,2,2,3,3,128]{5,2,4,3,1,0:T(2,128)} %param.6) | copy-start | bytes 442372
  6.4 17.4 %copy-start.1 = (f32[8,8,24,8]{2,3,1,0:T(8,128)S(1)}, f32[8,8,24,8]{2,3,1,0:T(8,128)}, u32[]{:S(2)}) copy-start(f32[8,8,24,8]{2,3,1,0:T(8,128)} %param.7) | copy-start | bytes 147460
  6.4 31.4 %all-to-all-start = ((f32[32,4,640]{2,1,0:T(4,128)}), f32[32,4,640]{2,1,0:T(4,128)S(1)}, u32[]{:S(2)}, u32[]{:S(2)}) async-start(f32[32,4,640]{2,1,0:T(4,128)} %pack.1), calls=%async_computation | async-start | bytes 655360 | tf_op jit(solution)/shard_map/all_to_all | solution.py:204
  37.8 0.7 copy-start
  48.2 14.6 %copy-start.2 = (f32[32,4,384]{2,1,0:T(4,128)S(1)}, f32[32,4,384]{2,1,0:T(4,128)}, u32[]{:S(2)}) copy-start(f32[32,4,384]{2,1,0:T(4,128)} %get-tuple-element.4) | copy-start | bytes 589828
  82.6 5.1 %copy-start.4 = (pred[384]{0:T(512)(128)(4,1)S(1)}, pred[384]{0:T(512)(128)(4,1)}, u32[]{:S(2)}) copy-start(pred[384]{0:T(512)(128)(4,1)} %constant.2.clone.1) | copy-start | bytes 1156
  82.6 12.2 %all-to-all-start.3 = ((f32[16,4,192]{2,1,0:T(4,128)}), f32[16,4,192]{2,1,0:T(4,128)S(1)}, u32[]{:S(2)}, u32[]{:S(2)}) async-start(f32[16,4,192]{2,1,0:T(4,128)} %broadcast_in_dim.5), calls=%async_computation.3 | async-start | bytes 131072 | tf_op jit(solution)/shard_map/all_to_all | solution.py:230

commit v2 on v1

--- a/solution.py
+++ b/solution.py
@@ -14,7 +14,7 @@
 
 
 def comp(ri, a, b):
-    return (ri * 3 + a) * 3 + b
+    return (a * 3 + b) * 2 + ri
 
 
 def product(left, right, dag_left=False, dag_right=False):
@@ -46,16 +46,14 @@
 
 
 def pack_kernel(links, field, cot, out, rows):
-    rows[...] = jnp.zeros_like(rows)
     for x in range(2):
         base = x * HALF
-        for ri in range(2):
-            for a in range(3):
-                first = comp(ri, a, 0)
-                rows[pl.ds(base + 288 + first, 3), :] = links[x, ri, a]
-                for c in range(C):
-                    rows[pl.ds(base + first * 8 + c, 3, stride=8), :] = field[c, x, ri, a]
-                    rows[pl.ds(base + 144 + first * 8 + c, 3, stride=8), :] = cot[c, x, ri, a]
+        for k in range(18):
+            rows[pl.ds(base + 8 * k, 8), :] = field[pl.ds(18 * x + k, C, stride=36), :]
+            rows[pl.ds(base + 144 + 8 * k, 8), :] = cot[pl.ds(18 * x + k, C, stride=36), :]
+        for k in range(9):
+            rows[pl.ds(base + 288 + 2 * k, 2), :] = links[x, k // 3, k % 3]
+        rows[pl.ds(base + 306, 14), :] = jnp.zeros((14, 128), jnp.float32)
     for block in range(5):
         turned = rows[pl.ds(128 * block, 128), :].T
         out[:, :, pl.ds(128 * block, 128)] = turned.reshape(32, 4, 128)
@@ -74,7 +72,7 @@
     def load_link(x):
         return [jnp.broadcast_to(rows[pl.ds(x * HALF + 288 + k, 1), :], shape) for k in range(18)]
 
-    one = [jnp.full(shape, 1.0 if k in (0, 4, 8) else 0.0, jnp.float32) for k in range(18)]
+    one = [jnp.full(shape, 1.0 if k in (0, 8, 16) else 0.0, jnp.float32) for k in range(18)]
     even = load_link(0)
     scan = product(even, load_link(1))
     step = 1
@@ -181,10 +179,8 @@
         turned = packed[:, :, pl.ds(128 * block, 128)].reshape(128, 128)
         rows[pl.ds(128 * block, 128), :] = turned.T
     for x in range(2):
-        for ri in range(2):
-            for a in range(3):
-                for c in range(C):
-                    out[c, x, ri, a] = rows[pl.ds(144 * x + comp(ri, a, 0) * 8 + c, 3, stride=8), :]
+        for k in range(18):
+            out[pl.ds(18 * x + k, C, stride=36), :] = rows[pl.ds(144 * x + 8 * k, 8), :]
 
 
 def per_device(gauge_links, in_field, cotangent, bilinear_weights):
@@ -195,12 +191,15 @@
     flat = bilinear_weights.reshape(C * C, width)
     weights = jnp.concatenate([jnp.pad(flat, ((0, 0), (0, 8))), jnp.pad(flat, ((0, 0), (8, 0)))], axis=0)
     vmem = lambda *shape: pltpu.VMEM(shape, f32)
+    grant = lambda mib: pltpu.CompilerParams(vmem_limit_bytes=mib << 20)
+    as_rows = lambda v: jnp.transpose(v, (0, 1, 3, 4, 2, 5)).reshape(-1, 128)
     packed = pl.pallas_call(
         pack_kernel,
         out_shape=jax.ShapeDtypeStruct((32, 4, 640), f32),
         scratch_shapes=[vmem(640, 128)],
+        compiler_params=grant(4),
         name="pack",
-    )(gauge_links, in_field, cotangent)
+    )(jnp.transpose(gauge_links, (0, 2, 3, 1, 4)), as_rows(in_field), as_rows(cotangent))
     packed = lax.all_to_all(packed, "gx", 0, 0, tiled=True)
     wide = 18 * 128
     grad_part, gw_part = pl.pallas_call(
@@ -218,6 +217,7 @@
             vmem(width + 8, wide),
             vmem(2, 18, 8, 128),
         ],
+        compiler_params=grant(14),
         name="layer",
     )(packed, weights)
     gw_part = lax.all_to_all(gw_part.reshape(n_yz, 64 // n_yz, width), "yz", 0, 0, tiled=True)
@@ -231,10 +231,12 @@
     back = jnp.pad(both[:, :, :288], ((0, 0), (0, 0), (0, 96)))
     grad_field = pl.pallas_call(
         unpack_kernel,
-        out_shape=jax.ShapeDtypeStruct(in_field.shape, f32),
+        out_shape=jax.ShapeDtypeStruct((288, 128), f32),
         scratch_shapes=[vmem(384, 128)],
+        compiler_params=grant(4),
         name="unpack",
     )(back)
+    grad_field = jnp.transpose(grad_field.reshape(C, 2, 3, 3, 2, 128), (0, 1, 4, 2, 3, 5))
     return (grad_field, grad_weights)
 
 

time: 97.1 us -> 91.2 us (0.939)
  local copies, waits for them, and re-layouts: 9.44 us -> 5.01 us
  waiting for transfers between devices: 15.6 us -> 19.6 us
  Pallas kernels: 12.6 us -> 8.72 us
  other arithmetic: 1.77 us -> 0.43 us
    unnamed x16 -> x12, local copies, waits for them, and re-layouts: 7.39 us -> 3.8 us
    all_to_all x1, waiting for transfers between devices: 2.88 us -> 6.18 us  [per_device(): lax.all_to_all(total, 'yz', 0, 0, tiled=True).reshape(C, C, lines, C)]
    pallas_call x1, Pallas kernels: 8.86 us -> 7.07 us  [per_device(): pl.pallas_call(functools.partial(layer_kernel, lines), out_shape=(jax.Sha...]
    pallas_call x1, Pallas kernels: 1.97 us -> 0.88 us  [per_device(): pl.pallas_call(pack_kernel, out_shape=jax.ShapeDtypeStruct((32, 4, 640),...]
  transfers between devices with their start and end apart: 2 -> 2, of which waited for: 2 -> 2; matrix products, arithmetic and copies ran while one was open for 4% -> 1% of each run, Pallas kernels for 2% -> 1%
where the time goes in v2:
time: 91.2 us; the launch traced here: 90.3 us
  blocking collectives  33.3 us (37%)
  starting transfers between devices  22.5 us (25%)
  waiting for transfers between devices  19.6 us (21%)
  Pallas kernels  8.72 us (10%)
  local copies, waits for them, and re-layouts  5.01 us (5%)
    all_to_all x1, blocking collectives, per_device(): both = lax.all_to_all(both, 'gx', 0, 0, tiled=True)  18.9 us
    all_to_all x1, starting transfers between devices, per_device(): packed = lax.all_to_all(packed, 'gx', 0, 0, tiled=True)  17.4 us
    all_to_all x1, blocking collectives, per_device(): lax.all_to_all(gw_part.reshape(n_yz, 64 // n_yz, width), 'yz', 0, 0, tile...  14.4 us
    all_to_all x1, waiting for transfers between devices, per_device(): packed = lax.all_to_all(packed, 'gx', 0, 0, tiled=True)  13.4 us
    pallas_call x1, Pallas kernels, per_device(): pl.pallas_call(functools.partial(layer_kernel, lines), out_shape=(jax.Sha...  7.07 us
    all_to_all x1, waiting for transfers between devices, per_device(): lax.all_to_all(total, 'yz', 0, 0, tiled=True).reshape(C, C, lines, C)  6.18 us
    all_to_all x1, starting transfers between devices, per_device(): lax.all_to_all(total, 'yz', 0, 0, tiled=True).reshape(C, C, lines, C)  5.14 us
    unnamed x12, local copies, waits for them, and re-layouts  3.8 us
  transfers between devices with their start and end apart: 2, of which 2 were waited for; matrix products, arithmetic and copies ran while one was open for 1% of the time, Pallas kernels for 1%

profile of v2, /device:TPU:1, one launch (start us, length us, event | category | flops | bytes accessed | tf_op | source)
XLA Modules:
  0.0 90.3 jit_solution(5085150381967585373)
XLA Ops:
  0.6 0.0 copy-start
  0.6 0.9 copy-done
  1.5 0.0 copy-start.1
  1.5 0.9 %copy-done.1 = f32[8,2,2,3,3,128]{5,2,4,3,1,0:T(2,128)S(1)} copy-done((f32[8,2,2,3,3,128]{5,2,4,3,1,0:T(2,128)S(1)}, f32[8,2,2,3,3,128]{5,2,4,3,1,0:T(2,128)}, u32[]{:S(2)}) %copy-start.1) | copy-done | bytes 147480
  2.5 0.0 copy-start.2
  2.5 0.7 copy-done.2
  3.2 0.9 pack.1
  4.1 0.0 copy-start.3
  4.1 17.4 %all-to-all-start = ((f32[32,4,640]{2,1,0:T(4,128)}), f32[32,4,640]{2,1,0:T(4,128)S(1)}, u32[]{:S(2)}, u32[]{:S(2)}) async-start(f32[32,4,640]{2,1,0:T(4,128)} %pack.1), calls=%async_computation | async-start | bytes 655360 | tf_op jit(solution)/shard_map/all_to_all | solution.py:203
  21.4 0.0 copy-done.3
  21.4 0.3 copy.7
  21.7 0.3 reshape.28
  22.0 0.1 select_maximum_fusion.weights
  22.1 13.4 %all-to-all-done.packed = f32[32,4,640]{2,1,0:T(4,128)S(1)} async-done(((f32[32,4,640]{2,1,0:T(4,128)}), f32[32,4,640]{2,1,0:T(4,128)S(1)}, u32[]{:S(2)}, u32[]{:S(2)}) %all-to-all-start) | async-done | bytes 327712 | tf_op jit(solution)/shard_map/all_to_all | solution.py:203
  35.5 7.1 %layer.1 = (f32[32,4,384]{2,1,0:T(4,128)S(1)}, f32[64,192]{1,0:T(8,128)S(1)}) custom-call(f32[32,4,640]{2,1,0:T(4,128)S(1)} %all-to-all-done.packed, f32[128,200]{1,0:T(8,128)S(1)} %select_maximum_fusion.weights), custom_call_target="tpu_custom_call" | custom-call | tf_op jit(solution)/shard_map/layer/pallas_call | solution.py:205
  42.6 14.4 %all_to_all.20 = f32[16,4,192]{2,1,0:T(4,128)S(1)} all-to-all(f32[16,4,192]{2,1,0:T(4,128)S(1)} %reshape.29), channel_id=1, replica_groups=mesh['gx'=32,'yz'=16] {'yz'}, dimensions={0} | all-to-all | bytes 98304 | tf_op jit(solution)/shard_map/all_to_all | solution.py:223
  57.0 0.1 pad_maximum_fusion
  57.2 18.9 %all_to_all.21 = f32[32,4,480]{2,1,0:T(4,128)S(1)} all-to-all(f32[32,4,480]{2,1,0:T(4,128)S(1)} %pad_maximum_fusion), channel_id=1, replica_groups=mesh['gx'=32,'yz'=16] {'gx'}, dimensions={0} | all-to-all | bytes 491520 | tf_op jit(solution)/shard_map/all_to_all | solution.py:226
  76.1 0.1 slice_reduce_fusion
  76.2 0.6 broadcast_in_dim.5
  76.9 0.0 copy-start.4
  76.9 5.1 %all-to-all-start.3 = ((f32[16,4,192]{2,1,0:T(4,128)}), f32[16,4,192]{2,1,0:T(4,128)S(1)}, u32[]{:S(2)}, u32[]{:S(2)}) async-start(f32[16,4,192]{2,1,0:T(4,128)} %broadcast_in_dim.5), calls=%async_computation.3 | async-start | bytes 131072 | tf_op jit(solution)/shard_map/all_to_all | solution.py:230
  82.0 0.0 copy-done.4
  82.1 0.8 unpack.1
  82.8 6.2 %all-to-all-done.3 = f32[16,4,192]{2,1,0:T(4,128)S(1)} async-done(((f32[16,4,192]{2,1,0:T(4,128)}), f32[16,4,192]{2,1,0:T(4,128)S(1)}, u32[]{:S(2)}, u32[]{:S(2)}) %all-to-all-start.3) | async-done | bytes 49184 | tf_op jit(solution)/shard_map/all_to_all | solution.py:230
  89.0 0.3 reshape.31
  89.3 1.0 %copy.8 = f32[8,8,24,8]{2,3,1,0:T(8,128)} copy(f32[8,8,24,8]{3,2,1,0:T(8,128)S(1)} %reshape.31) | data formatting | bytes 98304
  (5 shorter events, 0.1 us)
Async XLA Ops:
  0.6 0.9 %copy-start = (f32[8,2,2,3,3,128]{5,2,4,3,1,0:T(2,128)S(1)}, f32[8,2,2,3,3,128]{5,2,4,3,1,0:T(2,128)}, u32[]{:S(2)}) copy-start(f32[8,2,2,3,3,128]{5,2,4,3,1,0:T(2,128)} %param.5) | copy-start | bytes 442372
  1.5 0.9 %copy-start.1 = (f32[8,2,2,3,3,128]{5,2,4,3,1,0:T(2,128)S(1)}, f32[8,2,2,3,3,128]{5,2,4,3,1,0:T(2,128)}, u32[]{:S(2)}) copy-start(f32[8,2,2,3,3,128]{5,2,4,3,1,0:T(2,128)} %param.6) | copy-start | bytes 442372
  2.5 0.7 copy-start.2
  4.1 17.4 %copy-start.3 = (f32[8,8,24,8]{2,3,1,0:T(8,128)S(1)}, f32[8,8,24,8]{2,3,1,0:T(8,128)}, u32[]{:S(2)}) copy-start(f32[8,8,24,8]{2,3,1,0:T(8,128)} %param.7) | copy-start | bytes 147460
  4.1 31.4 %all-to-all-start = ((f32[32,4,640]{2,1,0:T(4,128)}), f32[32,4,640]{2,1,0:T(4,128)S(1)}, u32[]{:S(2)}, u32[]{:S(2)}) async-start(f32[32,4,640]{2,1,0:T(4,128)} %pack.1), calls=%async_computation | async-start | bytes 655360 | tf_op jit(solution)/shard_map/all_to_all | solution.py:203
  76.9 5.1 %copy-start.4 = (pred[384]{0:T(512)(128)(4,1)S(1)}, pred[384]{0:T(512)(128)(4,1)}, u32[]{:S(2)}) copy-start(pred[384]{0:T(512)(128)(4,1)} %constant.2.clone.1) | copy-start | bytes 1156
  76.9 12.2 %all-to-all-start.3 = ((f32[16,4,192]{2,1,0:T(4,128)}), f32[16,4,192]{2,1,0:T(4,128)S(1)}, u32[]{:S(2)}, u32[]{:S(2)}) async-start(f32[16,4,192]{2,1,0:T(4,128)} %broadcast_in_dim.5), calls=%async_computation.3 | async-start | bytes 131072 | tf_op jit(solution)/shard_map/all_to_all | solution.py:230

commit v3 on v2

--- a/solution.py
+++ b/solution.py
@@ -59,7 +59,35 @@
         out[:, :, pl.ds(128 * block, 128)] = turned.reshape(32, 4, 128)
 
 
-def layer_kernel(lines, packed, weights, grad_out, gw_out, rows, frame, wt, wp, gt, pair, windows, mixed, back, acc):
+KEPT = (128, 24, 16, 16, 16)
+
+
+def parts_of(state):
+    starts = [sum(KEPT[:n]) for n in range(len(KEPT))]
+    return [state.at[pl.ds(start, size), :] for start, size in zip(starts, KEPT)]
+
+
+def tile(ref, which, k):
+    return ref[pl.ds(8 * which, 8), pl.ds(128 * k, 128)]
+
+
+def put(ref, which, k, value):
+    ref[pl.ds(8 * which, 8), pl.ds(128 * k, 128)] = value
+
+
+def fill_windows(lines, wt, wp, windows):
+    lane = lax.broadcasted_iota(jnp.int32, (C, 128), 1)
+    for k in range(18):
+        for t in range(lines + 1):
+            x, m = (t + 1) % 2, (t + 1) // 2
+            value = tile(wt, x, k)
+            if m:
+                value = pltpu.roll(jnp.where(lane < 4 * m, tile(wp, x, k), value), 128 - 4 * m, 1)
+            put(windows, t, k, value)
+
+
+def forward_kernel(lines, packed, gw_out, state, rows, gt, windows):
+    pair, frame, gt_kept, wt, wp = parts_of(state)
     shape = (C, 128)
     lane = lax.broadcasted_iota(jnp.int32, shape, 1)
     for block in range(5):
@@ -83,52 +111,62 @@
         step *= 2
     for k in range(18):
         before = jnp.where(lane >= 4, pltpu.roll(scan[k], 4, 1), one[k])
-        frame[0, k] = before
+        put(frame, 0, k, before)
         whole = scan[k]
         reach = 1
         while reach < 32:
             whole = jnp.where(lane < 128 - 4 * reach, pltpu.roll(whole, 128 - 4 * reach, 1), whole)
             reach *= 2
-        frame[2, k] = whole
-    v_odd = product([frame[0, k] for k in range(18)], load_link(0))
+        put(frame, 2, k, whole)
+    def get_frame(which):
+        return [tile(frame, which, k) for k in range(18)]
+
+    v_odd = product(get_frame(0), load_link(0))
     for k in range(18):
-        frame[1, k] = v_odd[k]
-
-    def get_frame(which):
-        return [frame[which, k] for k in range(18)]
-
-    for x in range(2):
-        for offset, target in ((0, wt), (144, gt)):
-            turned = product(product(get_frame(x), load8(x, offset)), get_frame(x), dag_right=True)
-            for k in range(18):
-                target[x, k] = turned[k]
-        turned = product(product(get_frame(2), [wt[x, k] for k in range(18)]), get_frame(2), dag_right=True)
-        for k in range(18):
-            wp[x, k] = turned[k]
-
-    for k in range(18):
-        columns = pl.ds(128 * k, 128)
-        for t in range(lines + 1):
-            x, m = (t + 1) % 2, (t + 1) // 2
-            value = wt[x, k]
-            if m:
-                value = pltpu.roll(jnp.where(lane < 4 * m, wp[x, k], value), 128 - 4 * m, 1)
-            windows[pl.ds(8 * t, 8), columns] = value
-
-    def spread(x, i):
-        return [jnp.broadcast_to(gt[x, k, pl.ds(i, 1), :], shape) for k in range(18)]
+        put(frame, 1, k, v_odd[k])
+
+    for x in range(2):
+        turned = product(product(get_frame(x), load8(x, 144)), get_frame(x), dag_right=True)
+        for k in range(18):
+            put(gt_kept, x, k, turned[k])
+            gt[x, k] = turned[k]
+        turned = product(product(get_frame(x), load8(x, 0)), get_frame(x), dag_right=True)
+        for k in range(18):
+            put(wt, x, k, turned[k])
+        turned = product(product(get_frame(2), [tile(wt, x, k) for k in range(18)]), get_frame(2), dag_right=True)
+        for k in range(18):
+            put(wp, x, k, turned[k])
+
+    fill_windows(lines, wt, wp, windows)
 
     for x in range(2):
         @pl.loop(0, C)
         def _(i):
-            value = product([wt[x, k] for k in range(18)], spread(x, i), dag_left=True)
+            value = product([tile(wt, x, k) for k in range(18)], spread(gt, x, i), dag_left=True)
             for k in range(18):
                 pair[pl.ds(pl.multiple_of(64 * x + 8 * i, 8), 8), pl.ds(128 * k, 128)] = value[k]
 
     gw2 = lax.dot_general(pair[...], windows[...], (((1,), (1,)), ((), ())), precision=HIGHEST,
                           preferred_element_type=jnp.float32)
     width = lines * C
-    gw_out[...] = gw2[:64, :width] + gw2[64:, 8:8 + width]
+    gw_out[...] = (gw2[:64, :width] + gw2[64:, 8:8 + width]).reshape(gw_out.shape)
+
+
+def spread(source, x, i):
+    return [jnp.broadcast_to(source[x, k, pl.ds(i, 1), :], (C, 128)) for k in range(18)]
+
+
+def backward_kernel(lines, weights, state, grad_out, rows, mixed, back, acc, wrap, gt, windows):
+    pair, frame, gt_kept, wt, wp = parts_of(state)
+    fill_windows(lines, wt, wp, windows)
+    for x in range(2):
+        for k in range(18):
+            gt[x, k] = tile(gt_kept, x, k)
+    shape = (C, 128)
+    lane = lax.broadcasted_iota(jnp.int32, shape, 1)
+
+    def get_frame(which):
+        return [tile(frame, which, k) for k in range(18)]
 
     mixed[...] = jnp.dot(weights[...], windows[...], precision=HIGHEST, preferred_element_type=jnp.float32)
     back[...] = lax.dot_general(weights[...], pair[...], (((0,), (0,)), ((), ())), precision=HIGHEST,
@@ -151,17 +189,17 @@
                 else:
                     inside = inside + value
             acc[x, k] = inside
-            wp[x, k] = wrapped
-
-    for x in range(2):
-        turned = product(product(get_frame(2), [wp[x, k] for k in range(18)], dag_left=True), get_frame(2))
+            wrap[x, k] = wrapped
+
+    for x in range(2):
+        turned = product(product(get_frame(2), [wrap[x, k] for k in range(18)], dag_left=True), get_frame(2))
         for k in range(18):
             acc[x, k] = acc[x, k] + turned[k]
 
         @pl.loop(0, C)
         def _(i):
             here = [mixed[pl.ds(pl.multiple_of(64 * x + 8 * i, 8), 8), pl.ds(128 * k, 128)] for k in range(18)]
-            value = product(spread(x, i), here, dag_right=True)
+            value = product(spread(gt, x, i), here, dag_right=True)
             for k in range(18):
                 acc[x, k] = acc[x, k] + value[k]
 
@@ -202,25 +240,35 @@
     )(jnp.transpose(gauge_links, (0, 2, 3, 1, 4)), as_rows(in_field), as_rows(cotangent))
     packed = lax.all_to_all(packed, "gx", 0, 0, tiled=True)
     wide = 18 * 128
-    grad_part, gw_part = pl.pallas_call(
-        functools.partial(layer_kernel, lines),
-        out_shape=(jax.ShapeDtypeStruct((32, 4, 384), f32), jax.ShapeDtypeStruct((64, width), f32)),
+    shapes = lambda *dims: jax.ShapeDtypeStruct(dims, f32)
+    gw_part, state = pl.pallas_call(
+        functools.partial(forward_kernel, lines),
+        out_shape=(
+            shapes(n_yz, 64 // n_yz, width),
+            shapes(sum(KEPT), wide),
+        ),
+        scratch_shapes=[vmem(640, 128), vmem(2, 18, 8, 128), vmem(width + 8, wide)],
+        compiler_params=grant(12),
+        cost_estimate=pl.CostEstimate(flops=10**9, bytes_accessed=4 << 20, transcendentals=0),
+        name="forward",
+    )(packed)
+    grad_part = pl.pallas_call(
+        functools.partial(backward_kernel, lines),
+        out_shape=shapes(32, 4, 384),
         scratch_shapes=[
-            vmem(640, 128),
-            vmem(3, 18, 8, 128),
+            vmem(384, 128),
+            vmem(128, wide),
+            vmem(width + 8, wide),
             vmem(2, 18, 8, 128),
             vmem(2, 18, 8, 128),
             vmem(2, 18, 8, 128),
-            vmem(128, wide),
             vmem(width + 8, wide),
-            vmem(128, wide),
-            vmem(width + 8, wide),
-            vmem(2, 18, 8, 128),
         ],
         compiler_params=grant(14),
-        name="layer",
-    )(packed, weights)
-    gw_part = lax.all_to_all(gw_part.reshape(n_yz, 64 // n_yz, width), "yz", 0, 0, tiled=True)
+        cost_estimate=pl.CostEstimate(flops=2 * 10**9, bytes_accessed=4 << 20, transcendentals=0),
+        name="backward",
+    )(weights, state)
+    gw_part = lax.all_to_all(gw_part, "yz", 0, 0, tiled=True)
     gw_part = jnp.sum(gw_part, axis=0)
     both = jnp.concatenate([grad_part[:, :, :288], jnp.broadcast_to(gw_part[None], (n_gx,) + gw_part.shape)], axis=2)
     both = lax.all_to_all(both, "gx", 0, 0, tiled=True)

time: 91.2 us -> 88.9 us (0.975)
  blocking collectives: 33.3 us -> 18.9 us
  starting transfers between devices: 22.5 us -> 29.8 us
  waiting for transfers between devices: 19.6 us -> 21.9 us
  Pallas kernels: 8.72 us -> 10.1 us
  local copies, waits for them, and re-layouts: 5.01 us -> 5.94 us
    all_to_all x1 -> x0, blocking collectives: 14.4 us -> none  [per_device(): lax.all_to_all(gw_part.reshape(n_yz, 64 // n_yz, width), 'yz', 0, 0, tile...]
    all_to_all x0 -> x1, starting transfers between devices: none -> 7.62 us  [per_device(): gw_part = lax.all_to_all(gw_part, 'yz', 0, 0, tiled=True)]
    all_to_all x0 -> x1, waiting for transfers between devices: none -> 3.27 us  [per_device(): gw_part = lax.all_to_all(gw_part, 'yz', 0, 0, tiled=True)]
    pallas_call x1 -> x2, Pallas kernels: 7.07 us -> 8.48 us  [the longest x1 4.79 us: per_device(): pl.pallas_call(functools.partial(forward_kernel, lines), out_shape=(shape...]
    unnamed x12 -> x10, local copies, waits for them, and re-layouts: 3.8 us -> 4.75 us
    all_to_all x1, waiting for transfers between devices: 13.4 us -> 12.4 us  [per_device(): packed = lax.all_to_all(packed, 'gx', 0, 0, tiled=True)]
  transfers between devices with their start and end apart: 2 -> 3, of which waited for: 2 -> 3; matrix products, arithmetic and copies ran while one was open for 1% -> 2% of each run, Pallas kernels for 1% -> 5%
where the time goes in v3:
time: 88.9 us; the launch traced here: 87.9 us
  starting transfers between devices  29.8 us (34%)
  waiting for transfers between devices  21.9 us (25%)
  blocking collectives  18.9 us (21%)
  Pallas kernels  10.1 us (11%)
  local copies, waits for them, and re-layouts  5.94 us (7%)
    all_to_all x1, blocking collectives, per_device(): both = lax.all_to_all(both, 'gx', 0, 0, tiled=True)  18.9 us
    all_to_all x1, starting transfers between devices, per_device(): packed = lax.all_to_all(packed, 'gx', 0, 0, tiled=True)  17.2 us
    all_to_all x1, waiting for transfers between devices, per_device(): packed = lax.all_to_all(packed, 'gx', 0, 0, tiled=True)  12.4 us
    all_to_all x1, starting transfers between devices, per_device(): gw_part = lax.all_to_all(gw_part, 'yz', 0, 0, tiled=True)  7.62 us
    all_to_all x1, waiting for transfers between devices, per_device(): lax.all_to_all(total, 'yz', 0, 0, tiled=True).reshape(C, C, lines, C)  6.18 us
    all_to_all x1, starting transfers between devices, per_device(): lax.all_to_all(total, 'yz', 0, 0, tiled=True).reshape(C, C, lines, C)  5 us
    pallas_call x1, Pallas kernels, per_device(): pl.pallas_call(functools.partial(forward_kernel, lines), out_shape=(shape...  4.79 us
    unnamed x10, local copies, waits for them, and re-layouts  4.75 us
  transfers between devices with their start and end apart: 3, of which 3 were waited for; matrix products, arithmetic and copies ran while one was open for 2% of the time, Pallas kernels for 5%

profile of v3, /device:TPU:1, one launch (start us, length us, event | category | flops | bytes accessed | tf_op | source)
XLA Modules:
  0.0 87.9 jit_solution(11883013757807085057)
XLA Ops:
  0.6 0.0 copy-start
  0.6 0.9 %copy-done = f32[8,2,2,3,3,128]{5,2,4,3,1,0:T(2,128)S(1)} copy-done((f32[8,2,2,3,3,128]{5,2,4,3,1,0:T(2,128)S(1)}, f32[8,2,2,3,3,128]{5,2,4,3,1,0:T(2,128)}, u32[]{:S(2)}) %copy-start) | copy-done | bytes 147480
  1.5 0.0 copy-start.1
  1.5 0.9 %copy-done.1 = f32[8,2,2,3,3,128]{5,2,4,3,1,0:T(2,128)S(1)} copy-done((f32[8,2,2,3,3,128]{5,2,4,3,1,0:T(2,128)S(1)}, f32[8,2,2,3,3,128]{5,2,4,3,1,0:T(2,128)}, u32[]{:S(2)}) %copy-start.1) | copy-done | bytes 147480
  2.5 0.0 copy-start.2
  2.5 0.7 copy-done.2
  3.2 0.9 %pack.1 = f32[32,4,640]{2,1,0:T(4,128)} custom-call(f32[2,3,3,2,128]{4,3,2,1,0:T(2,128)S(1)} %bitcast.16, f32[288,128]{1,0:T(8,128)S(1)} %bitcast.14, f32[288,128]{1,0:T(8,128)S(1)} %bitcast.15), custom_call_target="tpu_custom_call" | custom-call | tf_op jit(solution)/shard_map/pack/pallas_call | solution.py:234
  4.1 17.2 %all-to-all-start = ((f32[32,4,640]{2,1,0:T(4,128)}), f32[32,4,640]{2,1,0:T(4,128)S(1)}, u32[]{:S(2)}, u32[]{:S(2)}) async-start(f32[32,4,640]{2,1,0:T(4,128)} %pack.1), calls=%async_computation | async-start | bytes 655360 | tf_op jit(solution)/shard_map/all_to_all | solution.py:241
  21.3 1.2 %copy.7 = f32[8,8,24,8]{3,2,1,0:T(8,128)S(1)} copy(f32[8,8,24,8]{2,3,1,0:T(8,128)} %param.7) | data formatting | bytes 98304 | tf_op args[3]
  22.5 0.3 reshape.23
  22.8 0.1 select_maximum_fusion.weights
  22.9 12.4 %all-to-all-done.packed = f32[32,4,640]{2,1,0:T(4,128)S(1)} async-done(((f32[32,4,640]{2,1,0:T(4,128)}), f32[32,4,640]{2,1,0:T(4,128)S(1)}, u32[]{:S(2)}, u32[]{:S(2)}) %all-to-all-start) | async-done | bytes 327712 | tf_op jit(solution)/shard_map/all_to_all | solution.py:241
  35.3 4.8 %forward.1 = (f32[16,4,192]{2,1,0:T(4,128)}, f32[200,2304]{1,0:T(8,128)S(1)}) custom-call(f32[32,4,640]{2,1,0:T(4,128)S(1)} %all-to-all-done.packed), custom_call_target="tpu_custom_call" | custom-call | flops 1000000000 | bytes 4194304 | tf_op jit(solution)/shard_map/forward/pallas_call | solution.py:244
  40.1 7.6 %all-to-all-start.1 = ((f32[16,4,192]{2,1,0:T(4,128)}), f32[16,4,192]{2,1,0:T(4,128)S(1)}, u32[]{:S(2)}, u32[]{:S(2)}) async-start(f32[16,4,192]{2,1,0:T(4,128)} %get-tuple-element.5), calls=%async_computation.1 | async-start | bytes 131072 | tf_op jit(solution)/shard_map/all_to_all | solution.py:271
  47.8 0.0 copy-start.3
  47.8 3.7 %backward.1 = f32[32,4,384]{2,1,0:T(4,128)S(1)} custom-call(f32[128,200]{1,0:T(8,128)S(1)} %select_maximum_fusion.weights, f32[200,2304]{1,0:T(8,128)S(1)} %get-tuple-element.4.state), custom_call_target="tpu_custom_call" | custom-call | flops 2000000000 | bytes 4194304 | tf_op jit(solution)/shard_map/backward/pallas_call | solution.py:255
  51.5 3.3 %all-to-all-done.1 = f32[16,4,192]{2,1,0:T(4,128)S(1)} async-done(((f32[16,4,192]{2,1,0:T(4,128)}), f32[16,4,192]{2,1,0:T(4,128)S(1)}, u32[]{:S(2)}, u32[]{:S(2)}) %all-to-all-start.1) | async-done | bytes 49184 | tf_op jit(solution)/shard_map/all_to_all | solution.py:271
  54.8 0.1 pad_maximum_fusion
  54.9 18.9 %all_to_all.20 = f32[32,4,480]{2,1,0:T(4,128)S(1)} all-to-all(f32[32,4,480]{2,1,0:T(4,128)S(1)} %pad_maximum_fusion), channel_id=1, replica_groups=mesh['gx'=32,'yz'=16] {'gx'}, dimensions={0} | all-to-all | bytes 491520 | tf_op jit(solution)/shard_map/all_to_all | solution.py:274
  73.8 0.1 slice_reduce_fusion
  74.0 0.6 broadcast_in_dim.5
  74.6 5.0 %all-to-all-start.3 = ((f32[16,4,192]{2,1,0:T(4,128)}), f32[16,4,192]{2,1,0:T(4,128)S(1)}, u32[]{:S(2)}, u32[]{:S(2)}) async-start(f32[16,4,192]{2,1,0:T(4,128)} %broadcast_in_dim.5), calls=%async_computation.3 | async-start | bytes 131072 | tf_op jit(solution)/shard_map/all_to_all | solution.py:278
  79.6 0.0 copy-done.3
  79.7 0.8 unpack.1
  80.5 6.2 %all-to-all-done.3 = f32[16,4,192]{2,1,0:T(4,128)S(1)} async-done(((f32[16,4,192]{2,1,0:T(4,128)}), f32[16,4,192]{2,1,0:T(4,128)S(1)}, u32[]{:S(2)}, u32[]{:S(2)}) %all-to-all-start.3) | async-done | bytes 49184 | tf_op jit(solution)/shard_map/all_to_all | solution.py:278
  86.7 0.3 reshape.27
  86.9 1.0 %copy.8 = f32[8,8,24,8]{2,3,1,0:T(8,128)} copy(f32[8,8,24,8]{3,2,1,0:T(8,128)S(1)} %reshape.27) | data formatting | bytes 98304
  (4 shorter events, 0.1 us)
Async XLA Ops:
  0.6 0.9 %copy-start = (f32[8,2,2,3,3,128]{5,2,4,3,1,0:T(2,128)S(1)}, f32[8,2,2,3,3,128]{5,2,4,3,1,0:T(2,128)}, u32[]{:S(2)}) copy-start(f32[8,2,2,3,3,128]{5,2,4,3,1,0:T(2,128)} %param.5) | copy-start | bytes 442372
  1.5 0.9 %copy-start.1 = (f32[8,2,2,3,3,128]{5,2,4,3,1,0:T(2,128)S(1)}, f32[8,2,2,3,3,128]{5,2,4,3,1,0:T(2,128)}, u32[]{:S(2)}) copy-start(f32[8,2,2,3,3,128]{5,2,4,3,1,0:T(2,128)} %param.6) | copy-start | bytes 442372
  2.5 0.7 copy-start.2
  4.1 31.3 %all-to-all-start = ((f32[32,4,640]{2,1,0:T(4,128)}), f32[32,4,640]{2,1,0:T(4,128)S(1)}, u32[]{:S(2)}, u32[]{:S(2)}) async-start(f32[32,4,640]{2,1,0:T(4,128)} %pack.1), calls=%async_computation | async-start | bytes 655360 | tf_op jit(solution)/shard_map/all_to_all | solution.py:241
  40.1 14.6 %all-to-all-start.1 = ((f32[16,4,192]{2,1,0:T(4,128)}), f32[16,4,192]{2,1,0:T(4,128)S(1)}, u32[]{:S(2)}, u32[]{:S(2)}) async-start(f32[16,4,192]{2,1,0:T(4,128)} %get-tuple-element.5), calls=%async_computation.1 | async-start | bytes 131072 | tf_op jit(solution)/shard_map/all_to_all | solution.py:271
  47.8 31.9 %copy-start.3 = (pred[384]{0:T(512)(128)(4,1)S(1)}, pred[384]{0:T(512)(128)(4,1)}, u32[]{:S(2)}) copy-start(pred[384]{0:T(512)(128)(4,1)} %constant.2.clone.1) | copy-start | bytes 1156
  74.6 12.0 %all-to-all-start.3 = ((f32[16,4,192]{2,1,0:T(4,128)}), f32[16,4,192]{2,1,0:T(4,128)S(1)}, u32[]{:S(2)}, u32[]{:S(2)}) async-start(f32[16,4,192]{2,1,0:T(4,128)} %broadcast_in_dim.5), calls=%async_computation.3 | async-start | bytes 131072 | tf_op jit(solution)/shard_map/all_to_all | solution.py:278

commit v4 on v3

--- a/solution.py
+++ b/solution.py
@@ -9,8 +9,8 @@
 from jax.sharding import PartitionSpec as P
 
 C = 8
+WHOLE = 67043328
 HALF = 320
-HIGHEST = lax.Precision.HIGHEST
 
 
 def comp(ri, a, b):
@@ -45,15 +45,38 @@
     return result
 
 
-def pack_kernel(links, field, cot, out, rows):
-    for x in range(2):
-        base = x * HALF
-        for k in range(18):
-            rows[pl.ds(base + 8 * k, 8), :] = field[pl.ds(18 * x + k, C, stride=36), :]
-            rows[pl.ds(base + 144 + 8 * k, 8), :] = cot[pl.ds(18 * x + k, C, stride=36), :]
+def halves(value):
+    high = value.astype(jnp.bfloat16)
+    return high, (value - high.astype(jnp.float32)).astype(jnp.bfloat16)
+
+
+def matmul(left, right, dims):
+    left_high, left_low = halves(left)
+    right_high, right_low = halves(right)
+    dot = functools.partial(lax.dot_general, dimension_numbers=(dims, ((), ())), preferred_element_type=jnp.float32)
+    return dot(left_high, right_high) + (dot(left_low, right_high) + dot(left_high, right_low))
+
+
+def pack_kernel(links_far, field_far, cot_far, out, links, field, cot, rows, sems):
+    copies = [
+        pltpu.make_async_copy(far, near, sems.at[n])
+        for n, (far, near) in enumerate(((field_far, field), (links_far, links), (cot_far, cot)))
+    ]
+    for copy in copies:
+        copy.start()
+    copies[0].wait()
+    for x in range(2):
+        rows[pl.ds(x * HALF + 306, 14), :] = jnp.zeros((14, 128), jnp.float32)
+        for k in range(18):
+            rows[pl.ds(x * HALF + 8 * k, 8), :] = field[pl.ds(18 * x + k, C, stride=36), :]
+    copies[1].wait()
+    for x in range(2):
         for k in range(9):
-            rows[pl.ds(base + 288 + 2 * k, 2), :] = links[x, k // 3, k % 3]
-        rows[pl.ds(base + 306, 14), :] = jnp.zeros((14, 128), jnp.float32)
+            rows[pl.ds(x * HALF + 288 + 2 * k, 2), :] = links[x, k // 3, k % 3]
+    copies[2].wait()
+    for x in range(2):
+        for k in range(18):
+            rows[pl.ds(x * HALF + 144 + 8 * k, 8), :] = cot[pl.ds(18 * x + k, C, stride=36), :]
     for block in range(5):
         turned = rows[pl.ds(128 * block, 128), :].T
         out[:, :, pl.ds(128 * block, 128)] = turned.reshape(32, 4, 128)
@@ -146,8 +169,7 @@
             for k in range(18):
                 pair[pl.ds(pl.multiple_of(64 * x + 8 * i, 8), 8), pl.ds(128 * k, 128)] = value[k]
 
-    gw2 = lax.dot_general(pair[...], windows[...], (((1,), (1,)), ((), ())), precision=HIGHEST,
-                          preferred_element_type=jnp.float32)
+    gw2 = matmul(pair[...], windows[...], ((1,), (1,)))
     width = lines * C
     gw_out[...] = (gw2[:64, :width] + gw2[64:, 8:8 + width]).reshape(gw_out.shape)
 
@@ -168,9 +190,8 @@
     def get_frame(which):
         return [tile(frame, which, k) for k in range(18)]
 
-    mixed[...] = jnp.dot(weights[...], windows[...], precision=HIGHEST, preferred_element_type=jnp.float32)
-    back[...] = lax.dot_general(weights[...], pair[...], (((0,), (0,)), ((), ())), precision=HIGHEST,
-                                preferred_element_type=jnp.float32)
+    mixed[...] = matmul(weights[...], windows[...], ((1,), (0,)))
+    back[...] = matmul(weights[...], pair[...], ((0,), (0,)))
 
     for k in range(18):
         columns = pl.ds(128 * k, 128)
@@ -234,8 +255,15 @@
     packed = pl.pallas_call(
         pack_kernel,
         out_shape=jax.ShapeDtypeStruct((32, 4, 640), f32),
-        scratch_shapes=[vmem(640, 128)],
-        compiler_params=grant(4),
+        in_specs=[pl.BlockSpec(memory_space=pltpu.HBM)] * 3,
+        scratch_shapes=[
+            vmem(2, 3, 3, 2, 128),
+            vmem(288, 128),
+            vmem(288, 128),
+            vmem(640, 128),
+            pltpu.SemaphoreType.DMA((3,)),
+        ],
+        compiler_params=pltpu.CompilerParams(vmem_limit_bytes=WHOLE),
         name="pack",
     )(jnp.transpose(gauge_links, (0, 2, 3, 1, 4)), as_rows(in_field), as_rows(cotangent))
     packed = lax.all_to_all(packed, "gx", 0, 0, tiled=True)

time: 88.9 us -> 86.5 us (0.973)
  local copies, waits for them, and re-layouts: 5.94 us -> 3.41 us
    unnamed x10 -> x4, local copies, waits for them, and re-layouts: 4.75 us -> 2.21 us
    pallas_call x1, Pallas kernels: 0.89 us -> 1.91 us  [per_device(): pl.pallas_call(pack_kernel, out_shape=jax.ShapeDtypeStruct((32, 4, 640),...]
  transfers between devices with their start and end apart: 3 -> 3, of which waited for: 3 -> 3; matrix products, arithmetic and copies ran while one was open for 2% -> 2% of each run, Pallas kernels for 5% -> 4%
where the time goes in v4:
time: 86.5 us; the launch traced here: 85.6 us
  starting transfers between devices  29.9 us (35%)
  waiting for transfers between devices  22.7 us (26%)
  blocking collectives  18.9 us (22%)
  Pallas kernels  9.53 us (11%)
  local copies, waits for them, and re-layouts  3.41 us (4%)
    all_to_all x1, blocking collectives, per_device(): both = lax.all_to_all(both, 'gx', 0, 0, tiled=True)  18.9 us
    all_to_all x1, starting transfers between devices, per_device(): packed = lax.all_to_all(packed, 'gx', 0, 0, tiled=True)  17.2 us
    all_to_all x1, waiting for transfers between devices, per_device(): packed = lax.all_to_all(packed, 'gx', 0, 0, tiled=True)  12.4 us
    all_to_all x1, starting transfers between devices, per_device(): gw_part = lax.all_to_all(gw_part, 'yz', 0, 0, tiled=True)  7.63 us
    all_to_all x1, waiting for transfers between devices, per_device(): lax.all_to_all(total, 'yz', 0, 0, tiled=True).reshape(C, C, lines, C)  6.18 us
    all_to_all x1, starting transfers between devices, per_device(): lax.all_to_all(total, 'yz', 0, 0, tiled=True).reshape(C, C, lines, C)  5 us
    all_to_all x1, waiting for transfers between devices, per_device(): gw_part = lax.all_to_all(gw_part, 'yz', 0, 0, tiled=True)  4.12 us
    pallas_call x1, Pallas kernels, per_device(): pl.pallas_call(functools.partial(forward_kernel, lines), out_shape=(shape...  3.99 us
  transfers between devices with their start and end apart: 3, of which 3 were waited for; matrix products, arithmetic and copies ran while one was open for 2% of the time, Pallas kernels for 4%

profile of v4, /device:TPU:1, one launch (start us, length us, event | category | flops | bytes accessed | tf_op | source)
XLA Modules:
  0.0 85.6 jit_solution(7007981767575296510)
XLA Ops:
  0.6 1.9 %pack.1 = f32[32,4,640]{2,1,0:T(4,128)} custom-call(f32[2,3,3,2,128]{4,3,2,1,0:T(2,128)} %bitcast.17, f32[288,128]{1,0:T(8,128)} %bitcast.14, f32[288,128]{1,0:T(8,128)} %bitcast.15), custom_call_target="tpu_custom_call" | custom-call | tf_op jit(solution)/shard_map/pack/pallas_call | solution.py:255
  2.5 17.2 %all-to-all-start = ((f32[32,4,640]{2,1,0:T(4,128)}), f32[32,4,640]{2,1,0:T(4,128)S(1)}, u32[]{:S(2)}, u32[]{:S(2)}) async-start(f32[32,4,640]{2,1,0:T(4,128)} %pack.1), calls=%async_computation | async-start | bytes 655360 | tf_op jit(solution)/shard_map/all_to_all | solution.py:269
  19.8 1.2 %copy.7 = f32[8,8,24,8]{3,2,1,0:T(8,128)S(1)} copy(f32[8,8,24,8]{2,3,1,0:T(8,128)} %param.7) | data formatting | bytes 98304 | tf_op args[3]
  21.0 0.3 reshape.23
  21.3 0.1 select_maximum_fusion.weights
  21.4 12.4 %all-to-all-done.packed = f32[32,4,640]{2,1,0:T(4,128)S(1)} async-done(((f32[32,4,640]{2,1,0:T(4,128)}), f32[32,4,640]{2,1,0:T(4,128)S(1)}, u32[]{:S(2)}, u32[]{:S(2)}) %all-to-all-start) | async-done | bytes 327712 | tf_op jit(solution)/shard_map/all_to_all | solution.py:269
  33.8 4.0 %forward.1 = (f32[16,4,192]{2,1,0:T(4,128)}, f32[200,2304]{1,0:T(8,128)S(1)}) custom-call(f32[32,4,640]{2,1,0:T(4,128)S(1)} %all-to-all-done.packed), custom_call_target="tpu_custom_call" | custom-call | flops 1000000000 | bytes 4194304 | tf_op jit(solution)/shard_map/forward/pallas_call | solution.py:272
  37.8 7.6 %all-to-all-start.1 = ((f32[16,4,192]{2,1,0:T(4,128)}), f32[16,4,192]{2,1,0:T(4,128)S(1)}, u32[]{:S(2)}, u32[]{:S(2)}) async-start(f32[16,4,192]{2,1,0:T(4,128)} %get-tuple-element.5), calls=%async_computation.1 | async-start | bytes 131072 | tf_op jit(solution)/shard_map/all_to_all | solution.py:299
  45.5 0.0 copy-start
  45.5 2.8 %backward.1 = f32[32,4,384]{2,1,0:T(4,128)S(1)} custom-call(f32[128,200]{1,0:T(8,128)S(1)} %select_maximum_fusion.weights, f32[200,2304]{1,0:T(8,128)S(1)} %get-tuple-element.4.state), custom_call_target="tpu_custom_call" | custom-call | flops 2000000000 | bytes 4194304 | tf_op jit(solution)/shard_map/backward/pallas_call | solution.py:283
  48.3 4.1 %all-to-all-done.1 = f32[16,4,192]{2,1,0:T(4,128)S(1)} async-done(((f32[16,4,192]{2,1,0:T(4,128)}), f32[16,4,192]{2,1,0:T(4,128)S(1)}, u32[]{:S(2)}, u32[]{:S(2)}) %all-to-all-start.1) | async-done | bytes 49184 | tf_op jit(solution)/shard_map/all_to_all | solution.py:299
  52.5 0.1 pad_maximum_fusion
  52.6 18.9 %all_to_all.20 = f32[32,4,480]{2,1,0:T(4,128)S(1)} all-to-all(f32[32,4,480]{2,1,0:T(4,128)S(1)} %pad_maximum_fusion), channel_id=1, replica_groups=mesh['gx'=32,'yz'=16] {'gx'}, dimensions={0} | all-to-all | bytes 491520 | tf_op jit(solution)/shard_map/all_to_all | solution.py:302
  71.5 0.1 slice_reduce_fusion
  71.7 0.6 broadcast_in_dim.5
  72.3 5.0 %all-to-all-start.3 = ((f32[16,4,192]{2,1,0:T(4,128)}), f32[16,4,192]{2,1,0:T(4,128)S(1)}, u32[]{:S(2)}, u32[]{:S(2)}) async-start(f32[16,4,192]{2,1,0:T(4,128)} %broadcast_in_dim.5), calls=%async_computation.3 | async-start | bytes 131072 | tf_op jit(solution)/shard_map/all_to_all | solution.py:306
  77.3 0.0 copy-done
  77.4 0.8 unpack.1
  78.2 6.2 %all-to-all-done.3 = f32[16,4,192]{2,1,0:T(4,128)S(1)} async-done(((f32[16,4,192]{2,1,0:T(4,128)}), f32[16,4,192]{2,1,0:T(4,128)S(1)}, u32[]{:S(2)}, u32[]{:S(2)}) %all-to-all-start.3) | async-done | bytes 49184 | tf_op jit(solution)/shard_map/all_to_all | solution.py:306
  84.4 0.3 reshape.27
  84.6 1.0 %copy.8 = f32[8,8,24,8]{2,3,1,0:T(8,128)} copy(f32[8,8,24,8]{3,2,1,0:T(8,128)S(1)} %reshape.27) | data formatting | bytes 98304
  (4 shorter events, 0.1 us)
Async XLA Ops:
  2.5 31.3 %all-to-all-start = ((f32[32,4,640]{2,1,0:T(4,128)}), f32[32,4,640]{2,1,0:T(4,128)S(1)}, u32[]{:S(2)}, u32[]{:S(2)}) async-start(f32[32,4,640]{2,1,0:T(4,128)} %pack.1), calls=%async_computation | async-start | bytes 655360 | tf_op jit(solution)/shard_map/all_to_all | solution.py:269
  37.8 14.6 %all-to-all-start.1 = ((f32[16,4,192]{2,1,0:T(4,128)}), f32[16,4,192]{2,1,0:T(4,128)S(1)}, u32[]{:S(2)}, u32[]{:S(2)}) async-start(f32[16,4,192]{2,1,0:T(4,128)} %get-tuple-element.5), calls=%async_computation.1 | async-start | bytes 131072 | tf_op jit(solution)/shard_map/all_to_all | solution.py:299
  45.5 31.9 %copy-start = (pred[384]{0:T(512)(128)(4,1)S(1)}, pred[384]{0:T(512)(128)(4,1)}, u32[]{:S(2)}) copy-start(pred[384]{0:T(512)(128)(4,1)} %constant.2.clone.1) | copy-start | bytes 1156
  72.3 12.0 %all-to-all-start.3 = ((f32[16,4,192]{2,1,0:T(4,128)}), f32[16,4,192]{2,1,0:T(4,128)S(1)}, u32[]{:S(2)}, u32[]{:S(2)}) async-start(f32[16,4,192]{2,1,0:T(4,128)} %broadcast_in_dim.5), calls=%async_computation.3 | async-start | bytes 131072 | tf_op jit(solution)/shard_map/all_to_all | solution.py:306

commit v5 on v4

--- a/solution.py
+++ b/solution.py
@@ -98,9 +98,9 @@
     ref[pl.ds(8 * which, 8), pl.ds(128 * k, 128)] = value
 
 
-def fill_windows(lines, wt, wp, windows):
+def fill_windows(lines, wt, wp, windows, entries=range(18)):
     lane = lax.broadcasted_iota(jnp.int32, (C, 128), 1)
-    for k in range(18):
+    for k in entries:
         for t in range(lines + 1):
             x, m = (t + 1) % 2, (t + 1) // 2
             value = tile(wt, x, k)
@@ -160,16 +160,17 @@
         for k in range(18):
             put(wp, x, k, turned[k])
 
-    fill_windows(lines, wt, wp, windows)
-
-    for x in range(2):
-        @pl.loop(0, C)
-        def _(i):
+    for x in range(2):
+        for i in range(C):
             value = product([tile(wt, x, k) for k in range(18)], spread(gt, x, i), dag_left=True)
             for k in range(18):
-                pair[pl.ds(pl.multiple_of(64 * x + 8 * i, 8), 8), pl.ds(128 * k, 128)] = value[k]
-
-    gw2 = matmul(pair[...], windows[...], ((1,), (1,)))
+                put(pair, 8 * x + i, k, value[k])
+    gw2 = None
+    for first in range(0, 18, 2):
+        fill_windows(lines, wt, wp, windows, range(first, first + 2))
+        columns = pl.ds(128 * first, 128 * 2)
+        part = matmul(pair[:, columns], windows[:, columns], ((1,), (1,)))
+        gw2 = part if gw2 is None else gw2 + part
     width = lines * C
     gw_out[...] = (gw2[:64, :width] + gw2[64:, 8:8 + width]).reshape(gw_out.shape)
 
@@ -190,8 +191,10 @@
     def get_frame(which):
         return [tile(frame, which, k) for k in range(18)]
 
-    mixed[...] = matmul(weights[...], windows[...], ((1,), (0,)))
-    back[...] = matmul(weights[...], pair[...], ((0,), (0,)))
+    for first in range(0, 18, 6):
+        columns = pl.ds(128 * first, 128 * 6)
+        mixed[:, columns] = matmul(weights[...], windows[:, columns], ((1,), (0,)))
+        back[:, columns] = matmul(weights[...], pair[:, columns], ((0,), (0,)))
 
     for k in range(18):
         columns = pl.ds(128 * k, 128)
@@ -217,9 +220,8 @@
         for k in range(18):
             acc[x, k] = acc[x, k] + turned[k]
 
-        @pl.loop(0, C)
-        def _(i):
-            here = [mixed[pl.ds(pl.multiple_of(64 * x + 8 * i, 8), 8), pl.ds(128 * k, 128)] for k in range(18)]
+        for i in range(C):
+            here = [tile(mixed, 8 * x + i, k) for k in range(18)]
             value = product(spread(gt, x, i), here, dag_right=True)
             for k in range(18):
                 acc[x, k] = acc[x, k] + value[k]

time: 86.5 us -> 85.5 us (0.988)
  Pallas kernels: 9.53 us -> 7.85 us
    pallas_call x1, Pallas kernels: 3.99 us -> 2.98 us  [per_device(): pl.pallas_call(functools.partial(forward_kernel, lines), out_shape=(shape...]
where the time goes in v5:
time: 85.5 us; the launch traced here: 84.6 us
  starting transfers between devices  29.9 us (35%)
  waiting for transfers between devices  23.4 us (27%)
  blocking collectives  18.9 us (22%)
  Pallas kernels  7.85 us (9%)
  local copies, waits for them, and re-layouts  3.41 us (4%)
    all_to_all x1, blocking collectives, per_device(): both = lax.all_to_all(both, 'gx', 0, 0, tiled=True)  18.9 us
    all_to_all x1, starting transfers between devices, per_device(): packed = lax.all_to_all(packed, 'gx', 0, 0, tiled=True)  17.2 us
    all_to_all x1, waiting for transfers between devices, per_device(): packed = lax.all_to_all(packed, 'gx', 0, 0, tiled=True)  12.4 us
    all_to_all x1, starting transfers between devices, per_device(): gw_part = lax.all_to_all(gw_part, 'yz', 0, 0, tiled=True)  7.62 us
    all_to_all x1, waiting for transfers between devices, per_device(): lax.all_to_all(total, 'yz', 0, 0, tiled=True).reshape(C, C, lines, C)  6.18 us
    all_to_all x1, starting transfers between devices, per_device(): lax.all_to_all(total, 'yz', 0, 0, tiled=True).reshape(C, C, lines, C)  5 us
    all_to_all x1, waiting for transfers between devices, per_device(): gw_part = lax.all_to_all(gw_part, 'yz', 0, 0, tiled=True)  4.77 us
    pallas_call x1, Pallas kernels, per_device(): pl.pallas_call(functools.partial(forward_kernel, lines), out_shape=(shape...  2.98 us
  transfers between devices with their start and end apart: 3, of which 3 were waited for; matrix products, arithmetic and copies ran while one was open for 2% of the time, Pallas kernels for 4%

profile of v5, /device:TPU:1, one launch (start us, length us, event | category | flops | bytes accessed | tf_op | source)
XLA Modules:
  0.0 84.6 jit_solution(4728585214419973024)
XLA Ops:
  0.6 1.9 %pack.1 = f32[32,4,640]{2,1,0:T(4,128)} custom-call(f32[2,3,3,2,128]{4,3,2,1,0:T(2,128)} %bitcast.17, f32[288,128]{1,0:T(8,128)} %bitcast.14, f32[288,128]{1,0:T(8,128)} %bitcast.15), custom_call_target="tpu_custom_call" | custom-call | tf_op jit(solution)/shard_map/pack/pallas_call | solution.py:257
  2.5 17.2 %all-to-all-start = ((f32[32,4,640]{2,1,0:T(4,128)}), f32[32,4,640]{2,1,0:T(4,128)S(1)}, u32[]{:S(2)}, u32[]{:S(2)}) async-start(f32[32,4,640]{2,1,0:T(4,128)} %pack.1), calls=%async_computation | async-start | bytes 655360 | tf_op jit(solution)/shard_map/all_to_all | solution.py:271
  19.8 1.2 %copy.7 = f32[8,8,24,8]{3,2,1,0:T(8,128)S(1)} copy(f32[8,8,24,8]{2,3,1,0:T(8,128)} %param.7) | data formatting | bytes 98304 | tf_op args[3]
  21.0 0.3 reshape.23
  21.3 0.1 select_maximum_fusion.weights
  21.4 12.4 %all-to-all-done.packed = f32[32,4,640]{2,1,0:T(4,128)S(1)} async-done(((f32[32,4,640]{2,1,0:T(4,128)}), f32[32,4,640]{2,1,0:T(4,128)S(1)}, u32[]{:S(2)}, u32[]{:S(2)}) %all-to-all-start) | async-done | bytes 327712 | tf_op jit(solution)/shard_map/all_to_all | solution.py:271
  33.8 3.0 %forward.1 = (f32[16,4,192]{2,1,0:T(4,128)}, f32[200,2304]{1,0:T(8,128)S(1)}) custom-call(f32[32,4,640]{2,1,0:T(4,128)S(1)} %all-to-all-done.packed), custom_call_target="tpu_custom_call" | custom-call | flops 1000000000 | bytes 4194304 | tf_op jit(solution)/shard_map/forward/pallas_call | solution.py:274
  36.8 7.6 %all-to-all-start.1 = ((f32[16,4,192]{2,1,0:T(4,128)}), f32[16,4,192]{2,1,0:T(4,128)S(1)}, u32[]{:S(2)}, u32[]{:S(2)}) async-start(f32[16,4,192]{2,1,0:T(4,128)} %get-tuple-element.5), calls=%async_computation.1 | async-start | bytes 131072 | tf_op jit(solution)/shard_map/all_to_all | solution.py:301
  44.4 0.0 copy-start
  44.4 2.2 %backward.1 = f32[32,4,384]{2,1,0:T(4,128)S(1)} custom-call(f32[128,200]{1,0:T(8,128)S(1)} %select_maximum_fusion.weights, f32[200,2304]{1,0:T(8,128)S(1)} %get-tuple-element.4.state), custom_call_target="tpu_custom_call" | custom-call | flops 2000000000 | bytes 4194304 | tf_op jit(solution)/shard_map/backward/pallas_call | solution.py:285
  46.6 4.8 %all-to-all-done.1 = f32[16,4,192]{2,1,0:T(4,128)S(1)} async-done(((f32[16,4,192]{2,1,0:T(4,128)}), f32[16,4,192]{2,1,0:T(4,128)S(1)}, u32[]{:S(2)}, u32[]{:S(2)}) %all-to-all-start.1) | async-done | bytes 49184 | tf_op jit(solution)/shard_map/all_to_all | solution.py:301
  51.5 0.1 pad_maximum_fusion
  51.6 18.9 %all_to_all.20 = f32[32,4,480]{2,1,0:T(4,128)S(1)} all-to-all(f32[32,4,480]{2,1,0:T(4,128)S(1)} %pad_maximum_fusion), channel_id=1, replica_groups=mesh['gx'=32,'yz'=16] {'gx'}, dimensions={0} | all-to-all | bytes 491520 | tf_op jit(solution)/shard_map/all_to_all | solution.py:304
  70.5 0.1 slice_reduce_fusion
  70.7 0.6 broadcast_in_dim.5
  71.3 5.0 %all-to-all-start.3 = ((f32[16,4,192]{2,1,0:T(4,128)}), f32[16,4,192]{2,1,0:T(4,128)S(1)}, u32[]{:S(2)}, u32[]{:S(2)}) async-start(f32[16,4,192]{2,1,0:T(4,128)} %broadcast_in_dim.5), calls=%async_computation.3 | async-start | bytes 131072 | tf_op jit(solution)/shard_map/all_to_all | solution.py:308
  76.3 0.0 copy-done
  76.4 0.8 unpack.1
  77.2 6.2 %all-to-all-done.3 = f32[16,4,192]{2,1,0:T(4,128)S(1)} async-done(((f32[16,4,192]{2,1,0:T(4,128)}), f32[16,4,192]{2,1,0:T(4,128)S(1)}, u32[]{:S(2)}, u32[]{:S(2)}) %all-to-all-start.3) | async-done | bytes 49184 | tf_op jit(solution)/shard_map/all_to_all | solution.py:308
  83.3 0.3 reshape.27
  83.6 1.0 %copy.8 = f32[8,8,24,8]{2,3,1,0:T(8,128)} copy(f32[8,8,24,8]{3,2,1,0:T(8,128)S(1)} %reshape.27) | data formatting | bytes 98304
  (4 shorter events, 0.1 us)
Async XLA Ops:
  2.5 31.3 %all-to-all-start = ((f32[32,4,640]{2,1,0:T(4,128)}), f32[32,4,640]{2,1,0:T(4,128)S(1)}, u32[]{:S(2)}, u32[]{:S(2)}) async-start(f32[32,4,640]{2,1,0:T(4,128)} %pack.1), calls=%async_computation | async-start | bytes 655360 | tf_op jit(solution)/shard_map/all_to_all | solution.py:271
  36.8 14.6 %all-to-all-start.1 = ((f32[16,4,192]{2,1,0:T(4,128)}), f32[16,4,192]{2,1,0:T(4,128)S(1)}, u32[]{:S(2)}, u32[]{:S(2)}) async-start(f32[16,4,192]{2,1,0:T(4,128)} %get-tuple-element.5), calls=%async_computation.1 | async-start | bytes 131072 | tf_op jit(solution)/shard_map/all_to_all | solution.py:301
  44.4 31.9 %copy-start = (pred[384]{0:T(512)(128)(4,1)S(1)}, pred[384]{0:T(512)(128)(4,1)}, u32[]{:S(2)}) copy-start(pred[384]{0:T(512)(128)(4,1)} %constant.2.clone.1) | copy-start | bytes 1156
  71.3 12.0 %all-to-all-start.3 = ((f32[16,4,192]{2,1,0:T(4,128)}), f32[16,4,192]{2,1,0:T(4,128)S(1)}, u32[]{:S(2)}, u32[]{:S(2)}) async-start(f32[16,4,192]{2,1,0:T(4,128)} %broadcast_in_dim.5), calls=%async_computation.3 | async-start | bytes 131072 | tf_op jit(solution)/shard_map/all_to_all | solution.py:308

commit v6 on v5

--- a/solution.py
+++ b/solution.py
@@ -82,7 +82,7 @@
         out[:, :, pl.ds(128 * block, 128)] = turned.reshape(32, 4, 128)
 
 
-KEPT = (128, 24, 16, 16, 16)
+KEPT = (128, 24, 16, 16)
 
 
 def parts_of(state):
@@ -109,8 +109,12 @@
             put(windows, t, k, value)
 
 
-def forward_kernel(lines, packed, gw_out, state, rows, gt, windows):
-    pair, frame, gt_kept, wt, wp = parts_of(state)
+def spread(source, x, i):
+    return [jnp.broadcast_to(source[x, k, pl.ds(i, 1), :], (C, 128)) for k in range(18)]
+
+
+def layer_kernel(lines, packed, weights, gw_out, grad_out, state, rows, gt, windows, mixed, back, acc, wrap):
+    pair, frame, wt, wp = parts_of(state)
     shape = (C, 128)
     lane = lax.broadcasted_iota(jnp.int32, shape, 1)
     for block in range(5):
@@ -151,7 +155,6 @@
     for x in range(2):
         turned = product(product(get_frame(x), load8(x, 144)), get_frame(x), dag_right=True)
         for k in range(18):
-            put(gt_kept, x, k, turned[k])
             gt[x, k] = turned[k]
         turned = product(product(get_frame(x), load8(x, 0)), get_frame(x), dag_right=True)
         for k in range(18):
@@ -173,23 +176,6 @@
         gw2 = part if gw2 is None else gw2 + part
     width = lines * C
     gw_out[...] = (gw2[:64, :width] + gw2[64:, 8:8 + width]).reshape(gw_out.shape)
-
-
-def spread(source, x, i):
-    return [jnp.broadcast_to(source[x, k, pl.ds(i, 1), :], (C, 128)) for k in range(18)]
-
-
-def backward_kernel(lines, weights, state, grad_out, rows, mixed, back, acc, wrap, gt, windows):
-    pair, frame, gt_kept, wt, wp = parts_of(state)
-    fill_windows(lines, wt, wp, windows)
-    for x in range(2):
-        for k in range(18):
-            gt[x, k] = tile(gt_kept, x, k)
-    shape = (C, 128)
-    lane = lax.broadcasted_iota(jnp.int32, shape, 1)
-
-    def get_frame(which):
-        return [tile(frame, which, k) for k in range(18)]
 
     for first in range(0, 18, 6):
         columns = pl.ds(128 * first, 128 * 6)
@@ -248,7 +234,10 @@
     lines = bilinear_weights.shape[2]
     width = lines * C
     f32 = jnp.float32
-    n_gx, n_yz = lax.axis_size("gx"), lax.axis_size("yz")
+    gx = ("yhi", "zc")
+    n_gx, n_yz, n_zc = lax.axis_size(gx), lax.axis_size("yz"), lax.axis_size("zc")
+    swap = lambda v, axes: lax.all_to_all(v, axes, 0, 0, tiled=True)
+    spread_over = lambda v, axes: jnp.broadcast_to(v[None], (lax.axis_size(axes),) + v.shape)
     flat = bilinear_weights.reshape(C * C, width)
     weights = jnp.concatenate([jnp.pad(flat, ((0, 0), (0, 8))), jnp.pad(flat, ((0, 0), (8, 0)))], axis=0)
     vmem = lambda *shape: pltpu.VMEM(shape, f32)
@@ -268,44 +257,30 @@
         compiler_params=pltpu.CompilerParams(vmem_limit_bytes=WHOLE),
         name="pack",
     )(jnp.transpose(gauge_links, (0, 2, 3, 1, 4)), as_rows(in_field), as_rows(cotangent))
-    packed = lax.all_to_all(packed, "gx", 0, 0, tiled=True)
+    packed, weights = lax.optimization_barrier((swap(packed, gx), weights))
     wide = 18 * 128
     shapes = lambda *dims: jax.ShapeDtypeStruct(dims, f32)
-    gw_part, state = pl.pallas_call(
-        functools.partial(forward_kernel, lines),
-        out_shape=(
-            shapes(n_yz, 64 // n_yz, width),
-            shapes(sum(KEPT), wide),
-        ),
-        scratch_shapes=[vmem(640, 128), vmem(2, 18, 8, 128), vmem(width + 8, wide)],
-        compiler_params=grant(12),
-        cost_estimate=pl.CostEstimate(flops=10**9, bytes_accessed=4 << 20, transcendentals=0),
-        name="forward",
-    )(packed)
-    grad_part = pl.pallas_call(
-        functools.partial(backward_kernel, lines),
-        out_shape=shapes(32, 4, 384),
+    gw_part, grad_part = pl.pallas_call(
+        functools.partial(layer_kernel, lines),
+        out_shape=(shapes(n_zc, 64 // n_zc, width), shapes(32, 4, 384)),
         scratch_shapes=[
-            vmem(384, 128),
+            vmem(sum(KEPT), wide),
+            vmem(640, 128),
+            vmem(2, 18, 8, 128),
+            vmem(width + 8, wide),
             vmem(128, wide),
             vmem(width + 8, wide),
             vmem(2, 18, 8, 128),
             vmem(2, 18, 8, 128),
-            vmem(2, 18, 8, 128),
-            vmem(width + 8, wide),
         ],
-        compiler_params=grant(14),
-        cost_estimate=pl.CostEstimate(flops=2 * 10**9, bytes_accessed=4 << 20, transcendentals=0),
-        name="backward",
-    )(weights, state)
-    gw_part = lax.all_to_all(gw_part, "yz", 0, 0, tiled=True)
-    gw_part = jnp.sum(gw_part, axis=0)
-    both = jnp.concatenate([grad_part[:, :, :288], jnp.broadcast_to(gw_part[None], (n_gx,) + gw_part.shape)], axis=2)
-    both = lax.all_to_all(both, "gx", 0, 0, tiled=True)
-    total = jnp.sum(both[:, :, 288:], axis=0)
+        compiler_params=grant(16),
+        cost_estimate=pl.CostEstimate(flops=3 * 10**9, bytes_accessed=4 << 20, transcendentals=0),
+        name="layer",
+    )(packed, weights)
+    both = swap(jnp.concatenate([grad_part[:, :, :288], jnp.concatenate([gw_part] * (n_gx // n_zc))], axis=2), gx)
+    total = jnp.sum(swap(spread_over(jnp.sum(both[:, :, 288:], axis=0), "yz"), "yz"), axis=0)
     scale = 1.0 / math.sqrt(100.0 * 2 * n_gx * 128 * n_yz)
-    total = jnp.broadcast_to((total * scale)[None], (n_yz,) + total.shape)
-    grad_weights = lax.all_to_all(total, "yz", 0, 0, tiled=True).reshape(C, C, lines, C)
+    grad_weights = swap(spread_over(total * scale, "zc"), "zc").reshape(C, C, lines, C)
     back = jnp.pad(both[:, :, :288], ((0, 0), (0, 0), (0, 96)))
     grad_field = pl.pallas_call(
         unpack_kernel,
@@ -319,16 +294,19 @@
 
 
 def solution(mesh):
+    n_gx, n_yz = mesh.devices.shape
+    split = jax.sharding.Mesh(mesh.devices.reshape(2, n_gx // 2, n_yz), ("yhi", "zc", "yz"))
+    gx = ("yhi", "zc")
     placed = (
-        P("gx", None, None, None, "yz"),
-        P(None, "gx", None, None, None, "yz"),
-        P(None, "gx", None, None, None, "yz"),
+        P(gx, None, None, None, "yz"),
+        P(None, gx, None, None, None, "yz"),
+        P(None, gx, None, None, None, "yz"),
         P(),
     )
     return jax.shard_map(
         per_device,
-        mesh=mesh,
+        mesh=split,
         in_specs=placed,
-        out_specs=(P(None, "gx", None, None, None, "yz"), P()),
+        out_specs=(P(None, gx, None, None, None, "yz"), P()),
         check_vma=False,
     )

time: 85.5 us -> 89.3 us (1.044)
  blocking collectives: 18.9 us -> 34.6 us
  starting transfers between devices: 29.9 us -> 23.7 us
  waiting for transfers between devices: 23.4 us -> 20.4 us
  Pallas kernels: 7.85 us -> 6.67 us
  local copies, waits for them, and re-layouts: 3.41 us -> 2.45 us
    all_to_all x1 -> x2, blocking collectives: 18.9 us -> 34.6 us  [per_device(): swap = lambda v, axes: lax.all_to_all(v, axes, 0, 0, tiled=True)]
    all_to_all x3 -> x2, starting transfers between devices: 29.9 us -> 23.7 us  [per_device(): swap = lambda v, axes: lax.all_to_all(v, axes, 0, 0, tiled=True)]
    all_to_all x3 -> x2, waiting for transfers between devices: 23.4 us -> 20.4 us  [per_device(): swap = lambda v, axes: lax.all_to_all(v, axes, 0, 0, tiled=True)]
    pallas_call x2 -> x1, Pallas kernels: 5.17 us -> 3.99 us  [per_device(): pl.pallas_call(functools.partial(layer_kernel, lines), out_shape=(shapes(...]
    unnamed x4 -> x6, local copies, waits for them, and re-layouts: 2.21 us -> 1.27 us
  transfers between devices with their start and end apart: 3 -> 2, of which waited for: 3 -> 2; matrix products, arithmetic and copies ran while one was open for 2% -> 1% of each run, Pallas kernels for 4% -> 1%
where the time goes in v6:
time: 89.3 us; the launch traced here: 88.9 us
  blocking collectives  34.6 us (39%)
  starting transfers between devices  23.7 us (27%)
  waiting for transfers between devices  20.4 us (23%)
  Pallas kernels  6.67 us (7%)
  local copies, waits for them, and re-layouts  2.45 us (3%)
    all_to_all x2, blocking collectives, per_device(): swap = lambda v, axes: lax.all_to_all(v, axes, 0, 0, tiled=True)  34.6 us
    all_to_all x2, starting transfers between devices, per_device(): swap = lambda v, axes: lax.all_to_all(v, axes, 0, 0, tiled=True)  23.7 us
    all_to_all x2, waiting for transfers between devices, per_device(): swap = lambda v, axes: lax.all_to_all(v, axes, 0, 0, tiled=True)  20.4 us
    pallas_call x1, Pallas kernels, per_device(): pl.pallas_call(functools.partial(layer_kernel, lines), out_shape=(shapes(...  3.99 us
    pallas_call x1, Pallas kernels, per_device(): pl.pallas_call(pack_kernel, out_shape=jax.ShapeDtypeStruct((32, 4, 640),...  1.91 us
  transfers between devices with their start and end apart: 2, of which 2 were waited for; matrix products, arithmetic and copies ran while one was open for 1% of the time, Pallas kernels for 1%

profile of v6, /device:TPU:1, one launch (start us, length us, event | category | flops | bytes accessed | tf_op | source)
XLA Modules:
  0.0 88.9 jit_solution(9419884813514614691)
XLA Ops:
  0.6 1.9 %pack.1 = f32[32,4,640]{2,1,0:T(4,128)} custom-call(f32[2,3,3,2,128]{4,3,2,1,0:T(2,128)} %bitcast.17, f32[288,128]{1,0:T(8,128)} %bitcast.14, f32[288,128]{1,0:T(8,128)} %bitcast.15), custom_call_target="tpu_custom_call" | custom-call | tf_op jit(solution)/shard_map/pack/pallas_call | solution.py:246
  2.5 0.0 copy-start
  2.6 17.4 %all-to-all-start = ((f32[32,4,640]{2,1,0:T(4,128)}), f32[32,4,640]{2,1,0:T(4,128)S(1)}, u32[]{:S(2)}, u32[]{:S(2)}) async-start(f32[32,4,640]{2,1,0:T(4,128)} %pack.1), calls=%async_computation | async-start | bytes 655360 | tf_op jit(solution)/shard_map/all_to_all | solution.py:239
  19.9 0.0 copy-done
  19.9 0.3 copy.11
  20.2 0.3 reshape.25
  20.5 0.1 select_maximum_fusion.weights
  20.6 13.4 %all-to-all-done.packed = f32[32,4,640]{2,1,0:T(4,128)S(1)} async-done(((f32[32,4,640]{2,1,0:T(4,128)}), f32[32,4,640]{2,1,0:T(4,128)S(1)}, u32[]{:S(2)}, u32[]{:S(2)}) %all-to-all-start) | async-done | bytes 327712 | tf_op jit(solution)/shard_map/all_to_all | solution.py:239
  34.0 4.0 %layer.1 = (f32[16,4,192]{2,1,0:T(4,128)S(1)}, f32[32,4,384]{2,1,0:T(4,128)S(1)}) custom-call(f32[32,4,640]{2,1,0:T(4,128)S(1)} %all-to-all-done.packed, f32[128,200]{1,0:T(8,128)S(1)} %select_maximum_fusion.weights), custom_call_target="tpu_custom_call" | custom-call | flops 3000000000 | bytes 4194304 | tf_op jit(solution)/shard_map/layer/pallas_call | solution.py:263
  38.0 0.1 maximum_maximum_fusion
  38.1 20.0 %all_to_all.20 = f32[32,4,480]{2,1,0:T(4,128)S(1)} all-to-all(f32[32,4,480]{2,1,0:T(4,128)S(1)} %maximum_maximum_fusion), channel_id=1, replica_groups=mesh['yhi'=2,'zc'=16,'yz'=16] {'yhi','zc'}, dimensions={0} | all-to-all | bytes 491520 | tf_op jit(solution)/shard_map/all_to_all | solution.py:239
  58.1 0.1 slice_reduce_fusion
  58.3 14.6 %all_to_all.21 = f32[16,4,192]{2,1,0:T(4,128)S(1)} all-to-all(f32[16,4,192]{2,1,0:T(4,128)S(1)} %broadcast_in_dim.4), channel_id=1, replica_groups=mesh['yhi'=2,'zc'=16,'yz'=16] {'yz'}, dimensions={0} | all-to-all | bytes 98304 | tf_op jit(solution)/shard_map/all_to_all | solution.py:239
  72.9 0.6 broadcast_in_dim.5
  73.5 0.0 copy-start.1
  73.5 6.3 %all-to-all-start.3 = ((f32[16,4,192]{2,1,0:T(4,128)}), f32[16,4,192]{2,1,0:T(4,128)S(1)}, u32[]{:S(2)}, u32[]{:S(2)}) async-start(f32[16,4,192]{2,1,0:T(4,128)} %broadcast_in_dim.5), calls=%async_computation.3 | async-start | bytes 131072 | tf_op jit(solution)/shard_map/all_to_all | solution.py:239
  79.9 0.0 copy-done.1
  79.9 0.8 unpack.1
  80.7 7.0 %all-to-all-done.3 = f32[16,4,192]{2,1,0:T(4,128)S(1)} async-done(((f32[16,4,192]{2,1,0:T(4,128)}), f32[16,4,192]{2,1,0:T(4,128)S(1)}, u32[]{:S(2)}, u32[]{:S(2)}) %all-to-all-start.3) | async-done | bytes 49184 | tf_op jit(solution)/shard_map/all_to_all | solution.py:239
  87.7 0.3 reshape.27
  88.0 1.0 %copy.13 = f32[8,8,24,8]{2,3,1,0:T(8,128)} copy(f32[8,8,24,8]{3,2,1,0:T(8,128)S(1)} %reshape.27) | data formatting | bytes 98304
  (4 shorter events, 0.1 us)
Async XLA Ops:
  2.5 17.4 %copy-start = (f32[8,8,24,8]{2,3,1,0:T(8,128)S(1)}, f32[8,8,24,8]{2,3,1,0:T(8,128)}, u32[]{:S(2)}) copy-start(f32[8,8,24,8]{2,3,1,0:T(8,128)} %param.7) | copy-start | bytes 147460
  2.6 31.4 %all-to-all-start = ((f32[32,4,640]{2,1,0:T(4,128)}), f32[32,4,640]{2,1,0:T(4,128)S(1)}, u32[]{:S(2)}, u32[]{:S(2)}) async-start(f32[32,4,640]{2,1,0:T(4,128)} %pack.1), calls=%async_computation | async-start | bytes 655360 | tf_op jit(solution)/shard_map/all_to_all | solution.py:239
  73.5 6.3 %copy-start.1 = (pred[384]{0:T(512)(128)(4,1)S(1)}, pred[384]{0:T(512)(128)(4,1)}, u32[]{:S(2)}) copy-start(pred[384]{0:T(512)(128)(4,1)} %constant.2.clone.1) | copy-start | bytes 1156
  73.5 14.2 %all-to-all-start.3 = ((f32[16,4,192]{2,1,0:T(4,128)}), f32[16,4,192]{2,1,0:T(4,128)S(1)}, u32[]{:S(2)}, u32[]{:S(2)}) async-start(f32[16,4,192]{2,1,0:T(4,128)} %broadcast_in_dim.5), calls=%async_computation.3 | async-start | bytes 131072 | tf_op jit(solution)/shard_map/all_to_all | solution.py:239

commit v7 on v5

--- a/solution.py
+++ b/solution.py
@@ -248,7 +248,8 @@
     lines = bilinear_weights.shape[2]
     width = lines * C
     f32 = jnp.float32
-    n_gx, n_yz = lax.axis_size("gx"), lax.axis_size("yz")
+    gx = ("zy", "core")
+    n_gx, n_yz = lax.axis_size(gx), lax.axis_size("yz")
     flat = bilinear_weights.reshape(C * C, width)
     weights = jnp.concatenate([jnp.pad(flat, ((0, 0), (0, 8))), jnp.pad(flat, ((0, 0), (8, 0)))], axis=0)
     vmem = lambda *shape: pltpu.VMEM(shape, f32)
@@ -268,7 +269,7 @@
         compiler_params=pltpu.CompilerParams(vmem_limit_bytes=WHOLE),
         name="pack",
     )(jnp.transpose(gauge_links, (0, 2, 3, 1, 4)), as_rows(in_field), as_rows(cotangent))
-    packed = lax.all_to_all(packed, "gx", 0, 0, tiled=True)
+    packed = lax.all_to_all(packed, gx, 0, 0, tiled=True)
     wide = 18 * 128
     shapes = lambda *dims: jax.ShapeDtypeStruct(dims, f32)
     gw_part, state = pl.pallas_call(
@@ -300,35 +301,42 @@
     )(weights, state)
     gw_part = lax.all_to_all(gw_part, "yz", 0, 0, tiled=True)
     gw_part = jnp.sum(gw_part, axis=0)
-    both = jnp.concatenate([grad_part[:, :, :288], jnp.broadcast_to(gw_part[None], (n_gx,) + gw_part.shape)], axis=2)
-    both = lax.all_to_all(both, "gx", 0, 0, tiled=True)
+    half = width // 2
+    to_first = lax.broadcasted_iota(jnp.int32, (n_gx, 4, half), 0) % 2 == 0
+    for_core = jnp.where(to_first, gw_part[None, :, :half], gw_part[None, :, half:])
+    both = jnp.concatenate([grad_part[:, :, :288], for_core], axis=2)
+    both = lax.all_to_all(both, gx, 0, 0, tiled=True)
     total = jnp.sum(both[:, :, 288:], axis=0)
     scale = 1.0 / math.sqrt(100.0 * 2 * n_gx * 128 * n_yz)
-    total = jnp.broadcast_to((total * scale)[None], (n_yz,) + total.shape)
-    grad_weights = lax.all_to_all(total, "yz", 0, 0, tiled=True).reshape(C, C, lines, C)
-    back = jnp.pad(both[:, :, :288], ((0, 0), (0, 0), (0, 96)))
+    total = jnp.broadcast_to((total * scale)[None], (2 * n_yz,) + total.shape)
+    total = lax.all_to_all(total, ("core", "yz"), 0, 0, tiled=True)
+    total = total.reshape(2, C, C, lines // 2, C)
+    grad_weights = jnp.concatenate([total[0], total[1]], axis=2)
     grad_field = pl.pallas_call(
         unpack_kernel,
         out_shape=jax.ShapeDtypeStruct((288, 128), f32),
         scratch_shapes=[vmem(384, 128)],
         compiler_params=grant(4),
         name="unpack",
-    )(back)
+    )(both)
     grad_field = jnp.transpose(grad_field.reshape(C, 2, 3, 3, 2, 128), (0, 1, 4, 2, 3, 5))
     return (grad_field, grad_weights)
 
 
 def solution(mesh):
+    n_gx, n_yz = mesh.devices.shape
+    split = jax.sharding.Mesh(mesh.devices.reshape(n_gx // 2, 2, n_yz), ("zy", "core", "yz"))
+    gx = ("zy", "core")
     placed = (
-        P("gx", None, None, None, "yz"),
-        P(None, "gx", None, None, None, "yz"),
-        P(None, "gx", None, None, None, "yz"),
+        P(gx, None, None, None, "yz"),
+        P(None, gx, None, None, None, "yz"),
+        P(None, gx, None, None, None, "yz"),
         P(),
     )
     return jax.shard_map(
         per_device,
-        mesh=mesh,
+        mesh=split,
         in_specs=placed,
-        out_specs=(P(None, "gx", None, None, None, "yz"), P()),
+        out_specs=(P(None, gx, None, None, None, "yz"), P()),
         check_vma=False,
     )

time: 85.5 us -> 87.1 us (1.019)
  starting transfers between devices: 29.9 us -> 30.9 us
  other arithmetic: 0.43 us -> 1.35 us
    squeeze x0 -> x4, local copies, waits for them, and re-layouts: none -> 1.36 us  [per_device(): grad_weights = jnp.concatenate([total[0], total[1]], axis=2)]
    all_to_all x2, starting transfers between devices: 22.2 us -> 23.3 us  [the longest x1 17.2 us: per_device(): packed = lax.all_to_all(packed, gx, 0, 0, tiled=True)]
    unnamed x4 -> x1, local copies, waits for them, and re-layouts: 2.21 us -> 1.24 us
  transfers between devices with their start and end apart: 3 -> 3, of which waited for: 3 -> 3; matrix products, arithmetic and copies ran while one was open for 2% -> 2% of each run, Pallas kernels for 4% -> 3%
where the time goes in v7:
time: 87.1 us; the launch traced here: 86.7 us
  starting transfers between devices  30.9 us (35%)
  waiting for transfers between devices  24 us (28%)
  blocking collectives  18.3 us (21%)
  Pallas kernels  7.84 us (9%)
  local copies, waits for them, and re-layouts  3.58 us (4%)
  other arithmetic  1.35 us (2%)
    all_to_all x1, blocking collectives, per_device(): both = lax.all_to_all(both, gx, 0, 0, tiled=True)  18.3 us
    all_to_all x1, starting transfers between devices, per_device(): packed = lax.all_to_all(packed, gx, 0, 0, tiled=True)  17.2 us
    all_to_all x1, waiting for transfers between devices, per_device(): packed = lax.all_to_all(packed, gx, 0, 0, tiled=True)  12.4 us
    all_to_all x1, starting transfers between devices, per_device(): gw_part = lax.all_to_all(gw_part, 'yz', 0, 0, tiled=True)  7.62 us
    all_to_all x1, waiting for transfers between devices, per_device(): total = lax.all_to_all(total, ('core', 'yz'), 0, 0, tiled=True)  6.81 us
    all_to_all x1, starting transfers between devices, per_device(): total = lax.all_to_all(total, ('core', 'yz'), 0, 0, tiled=True)  6.05 us
    all_to_all x1, waiting for transfers between devices, per_device(): gw_part = lax.all_to_all(gw_part, 'yz', 0, 0, tiled=True)  4.79 us
    pallas_call x1, Pallas kernels, per_device(): pl.pallas_call(functools.partial(forward_kernel, lines), out_shape=(shape...  2.98 us
  transfers between devices with their start and end apart: 3, of which 3 were waited for; matrix products, arithmetic and copies ran while one was open for 2% of the time, Pallas kernels for 3%

profile of v7, /device:TPU:1, one launch (start us, length us, event | category | flops | bytes accessed | tf_op | source)
XLA Modules:
  0.0 86.7 jit_solution(5758819253202510461)
XLA Ops:
  0.6 1.9 %pack.1 = f32[32,4,640]{2,1,0:T(4,128)} custom-call(f32[2,3,3,2,128]{4,3,2,1,0:T(2,128)} %bitcast.17, f32[288,128]{1,0:T(8,128)} %bitcast.14, f32[288,128]{1,0:T(8,128)} %bitcast.15), custom_call_target="tpu_custom_call" | custom-call | tf_op jit(solution)/shard_map/pack/pallas_call | solution.py:258
  2.5 17.2 %all-to-all-start = ((f32[32,4,640]{2,1,0:T(4,128)}), f32[32,4,640]{2,1,0:T(4,128)S(1)}, u32[]{:S(2)}, u32[]{:S(2)}) async-start(f32[32,4,640]{2,1,0:T(4,128)} %pack.1), calls=%async_computation | async-start | bytes 655360 | tf_op jit(solution)/shard_map/all_to_all | solution.py:272
  19.8 1.2 %copy.9 = f32[8,8,24,8]{3,2,1,0:T(8,128)S(1)} copy(f32[8,8,24,8]{2,3,1,0:T(8,128)} %param.7) | data formatting | bytes 98304 | tf_op args[3]
  21.0 0.3 reshape.26
  21.3 0.1 select_maximum_fusion.weights
  21.4 12.4 %all-to-all-done.packed = f32[32,4,640]{2,1,0:T(4,128)S(1)} async-done(((f32[32,4,640]{2,1,0:T(4,128)}), f32[32,4,640]{2,1,0:T(4,128)S(1)}, u32[]{:S(2)}, u32[]{:S(2)}) %all-to-all-start) | async-done | bytes 327712 | tf_op jit(solution)/shard_map/all_to_all | solution.py:272
  33.8 3.0 %forward.1 = (f32[16,4,192]{2,1,0:T(4,128)}, f32[200,2304]{1,0:T(8,128)S(1)}) custom-call(f32[32,4,640]{2,1,0:T(4,128)S(1)} %all-to-all-done.packed), custom_call_target="tpu_custom_call" | custom-call | flops 1000000000 | bytes 4194304 | tf_op jit(solution)/shard_map/forward/pallas_call | solution.py:275
  36.8 7.6 %all-to-all-start.1 = ((f32[16,4,192]{2,1,0:T(4,128)}), f32[16,4,192]{2,1,0:T(4,128)S(1)}, u32[]{:S(2)}, u32[]{:S(2)}) async-start(f32[16,4,192]{2,1,0:T(4,128)} %get-tuple-element.5), calls=%async_computation.1 | async-start | bytes 131072 | tf_op jit(solution)/shard_map/all_to_all | solution.py:302
  44.4 2.2 %backward.1 = f32[32,4,384]{2,1,0:T(4,128)S(1)} custom-call(f32[128,200]{1,0:T(8,128)S(1)} %select_maximum_fusion.weights, f32[200,2304]{1,0:T(8,128)S(1)} %get-tuple-element.4.state), custom_call_target="tpu_custom_call" | custom-call | flops 2000000000 | bytes 4194304 | tf_op jit(solution)/shard_map/backward/pallas_call | solution.py:286
  46.6 4.8 %all-to-all-done.1 = f32[16,4,192]{2,1,0:T(4,128)S(1)} async-done(((f32[16,4,192]{2,1,0:T(4,128)}), f32[16,4,192]{2,1,0:T(4,128)S(1)}, u32[]{:S(2)}, u32[]{:S(2)}) %all-to-all-start.1) | async-done | bytes 49184 | tf_op jit(solution)/shard_map/all_to_all | solution.py:302
  51.4 0.1 fusion.2
  51.5 0.2 fusion
  51.7 0.1 pad_maximum_fusion.1
  51.8 18.3 %all_to_all.20.packed = f32[32,4,384]{2,1,0:T(4,128)S(1)} all-to-all(f32[32,4,384]{2,1,0:T(4,128)S(1)} %pad_maximum_fusion.1), channel_id=1, replica_groups=mesh['zy'=16,'core'=2,'yz'=16] {'zy','core'}, dimensions={0} | all-to-all | bytes 393216 | tf_op jit(solution)/shard_map/all_to_all | solution.py:308
  70.1 0.1 slice_reduce_fusion
  70.2 0.6 broadcast_in_dim.26
  70.8 6.1 %all-to-all-start.3 = ((f32[32,4,96]{2,1,0:T(4,128)}), f32[32,4,96]{2,1,0:T(4,128)S(1)}, u32[]{:S(2)}, u32[]{:S(2)}) async-start(f32[32,4,96]{2,1,0:T(4,128)} %broadcast_in_dim.26), calls=%async_computation.3 | async-start | bytes 131072 | tf_op jit(solution)/shard_map/all_to_all | solution.py:312
  76.9 0.8 unpack.1
  77.6 6.8 %all-to-all-done.3 = f32[32,4,96]{2,1,0:T(4,128)S(1)} async-done(((f32[32,4,96]{2,1,0:T(4,128)}), f32[32,4,96]{2,1,0:T(4,128)S(1)}, u32[]{:S(2)}, u32[]{:S(2)}) %all-to-all-start.3) | async-done | bytes 49184 | tf_op jit(solution)/shard_map/all_to_all | solution.py:312
  84.5 0.2 squeeze.6
  84.7 0.4 copy.10
  85.1 0.2 squeeze.7
  85.4 0.4 copy.11
  85.8 0.8 pad_maximum_fusion
  (5 shorter events, 0.0 us)
Async XLA Ops:
  2.5 31.3 %all-to-all-start = ((f32[32,4,640]{2,1,0:T(4,128)}), f32[32,4,640]{2,1,0:T(4,128)S(1)}, u32[]{:S(2)}, u32[]{:S(2)}) async-start(f32[32,4,640]{2,1,0:T(4,128)} %pack.1), calls=%async_computation | async-start | bytes 655360 | tf_op jit(solution)/shard_map/all_to_all | solution.py:272
  36.8 14.6 %all-to-all-start.1 = ((f32[16,4,192]{2,1,0:T(4,128)}), f32[16,4,192]{2,1,0:T(4,128)S(1)}, u32[]{:S(2)}, u32[]{:S(2)}) async-start(f32[16,4,192]{2,1,0:T(4,128)} %get-tuple-element.5), calls=%async_computation.1 | async-start | bytes 131072 | tf_op jit(solution)/shard_map/all_to_all | solution.py:302
  70.8 13.6 %all-to-all-start.3 = ((f32[32,4,96]{2,1,0:T(4,128)}), f32[32,4,96]{2,1,0:T(4,128)S(1)}, u32[]{:S(2)}, u32[]{:S(2)}) async-start(f32[32,4,96]{2,1,0:T(4,128)} %broadcast_in_dim.26), calls=%async_computation.3 | async-start | bytes 131072 | tf_op jit(solution)/shard_map/all_to_all | solution.py:312

commit v8 on v7

--- a/solution.py
+++ b/solution.py
@@ -303,15 +303,14 @@
     gw_part = jnp.sum(gw_part, axis=0)
     half = width // 2
     to_first = lax.broadcasted_iota(jnp.int32, (n_gx, 4, half), 0) % 2 == 0
-    for_core = jnp.where(to_first, gw_part[None, :, :half], gw_part[None, :, half:])
+    gw_part = gw_part.reshape(8, half)
+    for_core = jnp.where(to_first, gw_part[None, :4], gw_part[None, 4:])
     both = jnp.concatenate([grad_part[:, :, :288], for_core], axis=2)
     both = lax.all_to_all(both, gx, 0, 0, tiled=True)
     total = jnp.sum(both[:, :, 288:], axis=0)
     scale = 1.0 / math.sqrt(100.0 * 2 * n_gx * 128 * n_yz)
     total = jnp.broadcast_to((total * scale)[None], (2 * n_yz,) + total.shape)
-    total = lax.all_to_all(total, ("core", "yz"), 0, 0, tiled=True)
-    total = total.reshape(2, C, C, lines // 2, C)
-    grad_weights = jnp.concatenate([total[0], total[1]], axis=2)
+    grad_weights = lax.all_to_all(total, ("yz", "core"), 0, 0, tiled=True).reshape(C, C, lines, C)
     grad_field = pl.pallas_call(
         unpack_kernel,
         out_shape=jax.ShapeDtypeStruct((288, 128), f32),

time: 87.1 us -> 86.4 us (level)
    squeeze x4 -> x0, local copies, waits for them, and re-layouts: 1.36 us -> none  [per_device(): grad_weights = jnp.concatenate([total[0], total[1]], axis=2)]
    unnamed x1 -> x2, local copies, waits for them, and re-layouts: 1.24 us -> 2.21 us
where the time goes in v8:
time: 86.4 us; the launch traced here: 86 us
  starting transfers between devices  30.9 us (36%)
  waiting for transfers between devices  24.2 us (28%)
  blocking collectives  18.2 us (21%)
  Pallas kernels  7.84 us (9%)
  local copies, waits for them, and re-layouts  3.54 us (4%)
    all_to_all x1, blocking collectives, per_device(): both = lax.all_to_all(both, gx, 0, 0, tiled=True)  18.2 us
    all_to_all x1, starting transfers between devices, per_device(): packed = lax.all_to_all(packed, gx, 0, 0, tiled=True)  17.2 us
    all_to_all x1, waiting for transfers between devices, per_device(): packed = lax.all_to_all(packed, gx, 0, 0, tiled=True)  12.4 us
    all_to_all x1, starting transfers between devices, per_device(): gw_part = lax.all_to_all(gw_part, 'yz', 0, 0, tiled=True)  7.63 us
    all_to_all x1, waiting for transfers between devices, per_device(): lax.all_to_all(total, ('yz', 'core'), 0, 0, tiled=True)  7.01 us
    all_to_all x1, starting transfers between devices, per_device(): lax.all_to_all(total, ('yz', 'core'), 0, 0, tiled=True)  6.05 us
    all_to_all x1, waiting for transfers between devices, per_device(): gw_part = lax.all_to_all(gw_part, 'yz', 0, 0, tiled=True)  4.79 us
    pallas_call x1, Pallas kernels, per_device(): pl.pallas_call(functools.partial(forward_kernel, lines), out_shape=(shape...  2.97 us
  transfers between devices with their start and end apart: 3, of which 3 were waited for; matrix products, arithmetic and copies ran while one was open for 2% of the time, Pallas kernels for 3%

profile of v8, /device:TPU:1, one launch (start us, length us, event | category | flops | bytes accessed | tf_op | source)
XLA Modules:
  0.0 86.0 jit_solution(7782621652887838568)
XLA Ops:
  0.6 1.9 %pack.1 = f32[32,4,640]{2,1,0:T(4,128)} custom-call(f32[2,3,3,2,128]{4,3,2,1,0:T(2,128)} %bitcast.17, f32[288,128]{1,0:T(8,128)} %bitcast.14, f32[288,128]{1,0:T(8,128)} %bitcast.15), custom_call_target="tpu_custom_call" | custom-call | tf_op jit(solution)/shard_map/pack/pallas_call | solution.py:258
  2.5 17.2 %all-to-all-start = ((f32[32,4,640]{2,1,0:T(4,128)}), f32[32,4,640]{2,1,0:T(4,128)S(1)}, u32[]{:S(2)}, u32[]{:S(2)}) async-start(f32[32,4,640]{2,1,0:T(4,128)} %pack.1), calls=%async_computation | async-start | bytes 655360 | tf_op jit(solution)/shard_map/all_to_all | solution.py:272
  19.8 1.2 %copy.7 = f32[8,8,24,8]{3,2,1,0:T(8,128)S(1)} copy(f32[8,8,24,8]{2,3,1,0:T(8,128)} %param.7) | data formatting | bytes 98304 | tf_op args[3]
  21.0 0.3 reshape.29
  21.3 0.1 select_maximum_fusion.weights
  21.4 12.4 %all-to-all-done.packed = f32[32,4,640]{2,1,0:T(4,128)S(1)} async-done(((f32[32,4,640]{2,1,0:T(4,128)}), f32[32,4,640]{2,1,0:T(4,128)S(1)}, u32[]{:S(2)}, u32[]{:S(2)}) %all-to-all-start) | async-done | bytes 327712 | tf_op jit(solution)/shard_map/all_to_all | solution.py:272
  33.8 3.0 %forward.1 = (f32[16,4,192]{2,1,0:T(4,128)}, f32[200,2304]{1,0:T(8,128)S(1)}) custom-call(f32[32,4,640]{2,1,0:T(4,128)S(1)} %all-to-all-done.packed), custom_call_target="tpu_custom_call" | custom-call | flops 1000000000 | bytes 4194304 | tf_op jit(solution)/shard_map/forward/pallas_call | solution.py:275
  36.8 7.6 %all-to-all-start.1 = ((f32[16,4,192]{2,1,0:T(4,128)}), f32[16,4,192]{2,1,0:T(4,128)S(1)}, u32[]{:S(2)}, u32[]{:S(2)}) async-start(f32[16,4,192]{2,1,0:T(4,128)} %get-tuple-element.5), calls=%async_computation.1 | async-start | bytes 131072 | tf_op jit(solution)/shard_map/all_to_all | solution.py:302
  44.4 2.2 %backward.1 = f32[32,4,384]{2,1,0:T(4,128)S(1)} custom-call(f32[128,200]{1,0:T(8,128)S(1)} %select_maximum_fusion.weights, f32[200,2304]{1,0:T(8,128)S(1)} %get-tuple-element.4.state), custom_call_target="tpu_custom_call" | custom-call | flops 2000000000 | bytes 4194304 | tf_op jit(solution)/shard_map/backward/pallas_call | solution.py:286
  46.6 4.8 %all-to-all-done.1 = f32[16,4,192]{2,1,0:T(4,128)S(1)} async-done(((f32[16,4,192]{2,1,0:T(4,128)}), f32[16,4,192]{2,1,0:T(4,128)S(1)}, u32[]{:S(2)}, u32[]{:S(2)}) %all-to-all-start.1) | async-done | bytes 49184 | tf_op jit(solution)/shard_map/all_to_all | solution.py:302
  51.5 0.1 broadcast_in_dim.28
  51.5 0.1 broadcast_in_dim.30
  51.6 0.2 fusion
  51.8 0.1 pad_maximum_fusion
  51.9 18.2 %all_to_all.20.packed = f32[32,4,384]{2,1,0:T(4,128)S(1)} all-to-all(f32[32,4,384]{2,1,0:T(4,128)S(1)} %pad_maximum_fusion), channel_id=1, replica_groups=mesh['zy'=16,'core'=2,'yz'=16] {'zy','core'}, dimensions={0} | all-to-all | bytes 393216 | tf_op jit(solution)/shard_map/all_to_all | solution.py:309
  70.2 0.1 slice_reduce_fusion
  70.3 0.6 broadcast_in_dim.32
  70.9 6.0 %all-to-all-start.3 = ((f32[32,4,96]{2,1,0:T(4,128)}), f32[32,4,96]{2,1,0:T(4,128)S(1)}, u32[]{:S(2)}, u32[]{:S(2)}) async-start(f32[32,4,96]{2,1,0:T(4,128)} %broadcast_in_dim.32), calls=%async_computation.3 | async-start | bytes 131072 | tf_op jit(solution)/shard_map/all_to_all | solution.py:313
  77.0 0.8 unpack.1
  77.7 7.0 %all-to-all-done.3 = f32[32,4,96]{2,1,0:T(4,128)S(1)} async-done(((f32[32,4,96]{2,1,0:T(4,128)}), f32[32,4,96]{2,1,0:T(4,128)S(1)}, u32[]{:S(2)}, u32[]{:S(2)}) %all-to-all-start.3) | async-done | bytes 49184 | tf_op jit(solution)/shard_map/all_to_all | solution.py:313
  84.8 0.3 reshape.33
  85.0 1.0 %copy.8 = f32[8,8,24,8]{2,3,1,0:T(8,128)} copy(f32[8,8,24,8]{3,2,1,0:T(8,128)S(1)} %reshape.33) | data formatting | bytes 98304
  (5 shorter events, 0.0 us)
Async XLA Ops:
  2.5 31.3 %all-to-all-start = ((f32[32,4,640]{2,1,0:T(4,128)}), f32[32,4,640]{2,1,0:T(4,128)S(1)}, u32[]{:S(2)}, u32[]{:S(2)}) async-start(f32[32,4,640]{2,1,0:T(4,128)} %pack.1), calls=%async_computation | async-start | bytes 655360 | tf_op jit(solution)/shard_map/all_to_all | solution.py:272
  36.8 14.6 %all-to-all-start.1 = ((f32[16,4,192]{2,1,0:T(4,128)}), f32[16,4,192]{2,1,0:T(4,128)S(1)}, u32[]{:S(2)}, u32[]{:S(2)}) async-start(f32[16,4,192]{2,1,0:T(4,128)} %get-tuple-element.5), calls=%async_computation.1 | async-start | bytes 131072 | tf_op jit(solution)/shard_map/all_to_all | solution.py:302
  70.9 13.8 %all-to-all-start.3 = ((f32[32,4,96]{2,1,0:T(4,128)}), f32[32,4,96]{2,1,0:T(4,128)S(1)}, u32[]{:S(2)}, u32[]{:S(2)}) async-start(f32[32,4,96]{2,1,0:T(4,128)} %broadcast_in_dim.32), calls=%async_computation.3 | async-start | bytes 131072 | tf_op jit(solution)/shard_map/all_to_all | solution.py:313

commit v9 on v5

--- a/solution.py
+++ b/solution.py
@@ -57,7 +57,7 @@
     return dot(left_high, right_high) + (dot(left_low, right_high) + dot(left_high, right_low))
 
 
-def pack_kernel(links_far, field_far, cot_far, out, links, field, cot, rows, sems):
+def pack_kernel(links_far, field_far, cot_far, out_far, links, field, cot, rows, out, sems, out_sems):
     copies = [
         pltpu.make_async_copy(far, near, sems.at[n])
         for n, (far, near) in enumerate(((field_far, field), (links_far, links), (cot_far, cot)))
@@ -77,9 +77,15 @@
     for x in range(2):
         for k in range(18):
             rows[pl.ds(x * HALF + 144 + 8 * k, 8), :] = cot[pl.ds(18 * x + k, C, stride=36), :]
+    sent = []
     for block in range(5):
         turned = rows[pl.ds(128 * block, 128), :].T
-        out[:, :, pl.ds(128 * block, 128)] = turned.reshape(32, 4, 128)
+        out[block] = turned.reshape(32, 4, 128)
+        there = out_far.at[:, :, pl.ds(128 * block, 128)]
+        sent.append(pltpu.make_async_copy(out.at[block], there, out_sems.at[block]))
+        sent[-1].start()
+    for copy in sent:
+        copy.wait()
 
 
 KEPT = (128, 24, 16, 16, 16)
@@ -258,12 +264,15 @@
         pack_kernel,
         out_shape=jax.ShapeDtypeStruct((32, 4, 640), f32),
         in_specs=[pl.BlockSpec(memory_space=pltpu.HBM)] * 3,
+        out_specs=pl.BlockSpec(memory_space=pltpu.HBM),
         scratch_shapes=[
             vmem(2, 3, 3, 2, 128),
             vmem(288, 128),
             vmem(288, 128),
             vmem(640, 128),
+            vmem(5, 32, 4, 128),
             pltpu.SemaphoreType.DMA((3,)),
+            pltpu.SemaphoreType.DMA((5,)),
         ],
         compiler_params=pltpu.CompilerParams(vmem_limit_bytes=WHOLE),
         name="pack",

time: 85.5 us -> 85.5 us (level)
  no operation moved by 1% of the time
where the time goes in v9:
time: 85.5 us; the launch traced here: 84.6 us
  starting transfers between devices  29.9 us (35%)
  waiting for transfers between devices  23.4 us (27%)
  blocking collectives  18.9 us (22%)
  Pallas kernels  7.89 us (9%)
  local copies, waits for them, and re-layouts  3.41 us (4%)
    all_to_all x1, blocking collectives, per_device(): both = lax.all_to_all(both, 'gx', 0, 0, tiled=True)  18.9 us
    all_to_all x1, starting transfers between devices, per_device(): packed = lax.all_to_all(packed, 'gx', 0, 0, tiled=True)  17.2 us
    all_to_all x1, waiting for transfers between devices, per_device(): packed = lax.all_to_all(packed, 'gx', 0, 0, tiled=True)  12.4 us
    all_to_all x1, starting transfers between devices, per_device(): gw_part = lax.all_to_all(gw_part, 'yz', 0, 0, tiled=True)  7.62 us
    all_to_all x1, waiting for transfers between devices, per_device(): lax.all_to_all(total, 'yz', 0, 0, tiled=True).reshape(C, C, lines, C)  6.18 us
    all_to_all x1, starting transfers between devices, per_device(): lax.all_to_all(total, 'yz', 0, 0, tiled=True).reshape(C, C, lines, C)  5 us
    all_to_all x1, waiting for transfers between devices, per_device(): gw_part = lax.all_to_all(gw_part, 'yz', 0, 0, tiled=True)  4.77 us
    pallas_call x1, Pallas kernels, per_device(): pl.pallas_call(functools.partial(forward_kernel, lines), out_shape=(shape...  2.98 us
  transfers between devices with their start and end apart: 3, of which 3 were waited for; matrix products, arithmetic and copies ran while one was open for 2% of the time, Pallas kernels for 4%

profile of v9, /device:TPU:1, one launch (start us, length us, event | category | flops | bytes accessed | tf_op | source)
XLA Modules:
  0.0 84.6 jit_solution(7760525862428252783)
XLA Ops:
  0.6 1.9 %pack.1 = f32[32,4,640]{2,1,0:T(4,128)} custom-call(f32[2,3,3,2,128]{4,3,2,1,0:T(2,128)} %bitcast.17, f32[288,128]{1,0:T(8,128)} %bitcast.14, f32[288,128]{1,0:T(8,128)} %bitcast.15), custom_call_target="tpu_custom_call" | custom-call | tf_op jit(solution)/shard_map/pack/pallas_call | solution.py:263
  2.6 17.2 %all-to-all-start = ((f32[32,4,640]{2,1,0:T(4,128)}), f32[32,4,640]{2,1,0:T(4,128)S(1)}, u32[]{:S(2)}, u32[]{:S(2)}) async-start(f32[32,4,640]{2,1,0:T(4,128)} %pack.1), calls=%async_computation | async-start | bytes 655360 | tf_op jit(solution)/shard_map/all_to_all | solution.py:280
  19.8 1.2 %copy.7 = f32[8,8,24,8]{3,2,1,0:T(8,128)S(1)} copy(f32[8,8,24,8]{2,3,1,0:T(8,128)} %param.7) | data formatting | bytes 98304 | tf_op args[3]
  21.1 0.3 reshape.23
  21.3 0.1 select_maximum_fusion.weights
  21.4 12.4 %all-to-all-done.packed = f32[32,4,640]{2,1,0:T(4,128)S(1)} async-done(((f32[32,4,640]{2,1,0:T(4,128)}), f32[32,4,640]{2,1,0:T(4,128)S(1)}, u32[]{:S(2)}, u32[]{:S(2)}) %all-to-all-start) | async-done | bytes 327712 | tf_op jit(solution)/shard_map/all_to_all | solution.py:280
  33.9 3.0 %forward.1 = (f32[16,4,192]{2,1,0:T(4,128)}, f32[200,2304]{1,0:T(8,128)S(1)}) custom-call(f32[32,4,640]{2,1,0:T(4,128)S(1)} %all-to-all-done.packed), custom_call_target="tpu_custom_call" | custom-call | flops 1000000000 | bytes 4194304 | tf_op jit(solution)/shard_map/forward/pallas_call | solution.py:283
  36.8 7.6 %all-to-all-start.1 = ((f32[16,4,192]{2,1,0:T(4,128)}), f32[16,4,192]{2,1,0:T(4,128)S(1)}, u32[]{:S(2)}, u32[]{:S(2)}) async-start(f32[16,4,192]{2,1,0:T(4,128)} %get-tuple-element.5), calls=%async_computation.1 | async-start | bytes 131072 | tf_op jit(solution)/shard_map/all_to_all | solution.py:310
  44.5 0.0 copy-start
  44.5 2.2 %backward.1 = f32[32,4,384]{2,1,0:T(4,128)S(1)} custom-call(f32[128,200]{1,0:T(8,128)S(1)} %select_maximum_fusion.weights, f32[200,2304]{1,0:T(8,128)S(1)} %get-tuple-element.4.state), custom_call_target="tpu_custom_call" | custom-call | flops 2000000000 | bytes 4194304 | tf_op jit(solution)/shard_map/backward/pallas_call | solution.py:294
  46.7 4.8 %all-to-all-done.1 = f32[16,4,192]{2,1,0:T(4,128)S(1)} async-done(((f32[16,4,192]{2,1,0:T(4,128)}), f32[16,4,192]{2,1,0:T(4,128)S(1)}, u32[]{:S(2)}, u32[]{:S(2)}) %all-to-all-start.1) | async-done | bytes 49184 | tf_op jit(solution)/shard_map/all_to_all | solution.py:310
  51.5 0.1 pad_maximum_fusion
  51.6 18.9 %all_to_all.20 = f32[32,4,480]{2,1,0:T(4,128)S(1)} all-to-all(f32[32,4,480]{2,1,0:T(4,128)S(1)} %pad_maximum_fusion), channel_id=1, replica_groups=mesh['gx'=32,'yz'=16] {'gx'}, dimensions={0} | all-to-all | bytes 491520 | tf_op jit(solution)/shard_map/all_to_all | solution.py:313
  70.5 0.1 slice_reduce_fusion
  70.7 0.6 broadcast_in_dim.5
  71.3 5.0 %all-to-all-start.3 = ((f32[16,4,192]{2,1,0:T(4,128)}), f32[16,4,192]{2,1,0:T(4,128)S(1)}, u32[]{:S(2)}, u32[]{:S(2)}) async-start(f32[16,4,192]{2,1,0:T(4,128)} %broadcast_in_dim.5), calls=%async_computation.3 | async-start | bytes 131072 | tf_op jit(solution)/shard_map/all_to_all | solution.py:317
  76.4 0.0 copy-done
  76.4 0.8 unpack.1
  77.2 6.2 %all-to-all-done.3 = f32[16,4,192]{2,1,0:T(4,128)S(1)} async-done(((f32[16,4,192]{2,1,0:T(4,128)}), f32[16,4,192]{2,1,0:T(4,128)S(1)}, u32[]{:S(2)}, u32[]{:S(2)}) %all-to-all-start.3) | async-done | bytes 49184 | tf_op jit(solution)/shard_map/all_to_all | solution.py:317
  83.4 0.3 reshape.27
  83.6 1.0 %copy.8 = f32[8,8,24,8]{2,3,1,0:T(8,128)} copy(f32[8,8,24,8]{3,2,1,0:T(8,128)S(1)} %reshape.27) | data formatting | bytes 98304
  (4 shorter events, 0.1 us)
Async XLA Ops:
  2.6 31.3 %all-to-all-start = ((f32[32,4,640]{2,1,0:T(4,128)}), f32[32,4,640]{2,1,0:T(4,128)S(1)}, u32[]{:S(2)}, u32[]{:S(2)}) async-start(f32[32,4,640]{2,1,0:T(4,128)} %pack.1), calls=%async_computation | async-start | bytes 655360 | tf_op jit(solution)/shard_map/all_to_all | solution.py:280
  36.8 14.6 %all-to-all-start.1 = ((f32[16,4,192]{2,1,0:T(4,128)}), f32[16,4,192]{2,1,0:T(4,128)S(1)}, u32[]{:S(2)}, u32[]{:S(2)}) async-start(f32[16,4,192]{2,1,0:T(4,128)} %get-tuple-element.5), calls=%async_computation.1 | async-start | bytes 131072 | tf_op jit(solution)/shard_map/all_to_all | solution.py:310
  44.5 31.9 %copy-start = (pred[384]{0:T(512)(128)(4,1)S(1)}, pred[384]{0:T(512)(128)(4,1)}, u32[]{:S(2)}) copy-start(pred[384]{0:T(512)(128)(4,1)} %constant.2.clone.1) | copy-start | bytes 1156
  71.3 12.0 %all-to-all-start.3 = ((f32[16,4,192]{2,1,0:T(4,128)}), f32[16,4,192]{2,1,0:T(4,128)S(1)}, u32[]{:S(2)}, u32[]{:S(2)}) async-start(f32[16,4,192]{2,1,0:T(4,128)} %broadcast_in_dim.5), calls=%async_computation.3 | async-start | bytes 131072 | tf_op jit(solution)/shard_map/all_to_all | solution.py:317
